TPU v7x, 32 devices: a whole 2x2x4 slice. The times are simulated.
32 devices in a mesh: fsdp: 4 (over y, x), ctx: 4 (over z), tp: 2 (over core).
Axes of the slice: x: 2, y: 2, z: 4, core: 2. Of those that a mesh axis runs over, the one named last changes fastest.
Arguments:
- tokens: bfloat16 [2, 2, 4, 128, 2304], P(None, None, 'ctx', 'fsdp'), may hold values from -6 to 6
- segments: int32 [2, 2, 4, 128], P(None, None, 'ctx', 'fsdp'), may hold values from 0 to 3, as said below
- stretch_order: int32 [4], replicated, may hold values from 0 to 3, as said below
- norm_gains: float32 [4, 2304], replicated, may hold values from 0.25 to 1.75
- query_proj: bfloat16 [2304, 2048], P('fsdp', 'tp'), may hold values from -0.125 to 0.125
- keyval_proj: bfloat16 [2304, 2, 1024], P('fsdp', None, 'tp'), may hold values from -0.125 to 0.125
- attn_proj: bfloat16 [2304, 2048], P('fsdp', 'tp'), may hold values from -0.125 to 0.125
- ffn_in: bfloat16 [2304, 2, 9216], P('fsdp', None, 'tp'), may hold values from -0.125 to 0.125
- ffn_out: bfloat16 [2304, 9216], P('fsdp', 'tp'), may hold values from -0.0625 to 0.0625
- cotangent: bfloat16 [2, 2, 4, 128, 2304], P(None, None, 'ctx', 'fsdp'), may hold values from -6 to 6
Outputs:
- result: bfloat16 [2, 2, 4, 128, 2304], P(None, None, 'ctx', 'fsdp')
- grad_tokens: float32 [2, 2, 4, 128, 2304], P(None, None, 'ctx', 'fsdp')
- grad_gains: float32 [4, 2304], replicated
- grad_query: float32 [2304, 2048], P('fsdp', 'tp')
- grad_keyval: float32 [2304, 2, 1024], P('fsdp', None, 'tp')
- grad_attn: float32 [2304, 2048], P('fsdp', 'tp')
- grad_ffn_in: float32 [2304, 2, 9216], P('fsdp', None, 'tp')
- grad_ffn_out: float32 [2304, 9216], P('fsdp', 'tp')
Inputs may be any that keep to these rules, and one draw needn't show every extreme that they name: `segments`: along the positions of a sequence the segment ids never fall; every sequence holds exactly four documents, ids 0 to 3. Each of 0 to 3 once; slot c holds position blocks stretch_order[c] and 7 - stretch_order[c] of every sequence.
All inputs are finite; a program needn't handle non-finite values.
Results may differ from a plain program's by a relative error of at most 0.015.
Values may be sent and summed in bfloat16 or wider, within the bound.
No kernel may reach another device: no remote copies, remote signals or barrier semaphores. Data moves between devices by JAX's collectives and lax.ppermute only.
A program may use at most 640 MiB of HBM per device.

v0:
```python
import jax
import jax.numpy as jnp
from jax import lax
from jax.sharding import PartitionSpec as P

HEAD_DIM = 256


SOFT_CAP = 50.0
NORM_EPS = 1e-06


def rms_factor(values):
    return lax.rsqrt(jnp.mean(values * values, axis=-1, keepdims=True) + NORM_EPS)


def norm_back(grad_out, values, scale_gain):
    factor = rms_factor(values)
    normed = values * factor
    grad_gain = jnp.sum(grad_out * normed, axis=0)
    scaled_grad = grad_out * scale_gain
    grad_in = factor * (
        scaled_grad - normed * jnp.mean(scaled_grad * normed, axis=-1, keepdims=True)
    )
    return (grad_in, grad_gain)


def gelu_parts(gate_vals):
    values, pullback = jax.vjp(lambda inputs: jax.nn.gelu(inputs, approximate=True), gate_vals)
    return (values, pullback(jnp.ones_like(gate_vals))[0])


def dot_nt(left, right):
    return lax.dot_general(
        left, right, (((1,), (1,)), ((), ())), preferred_element_type=jnp.float32
    )


def dot_tn(left, right):
    return lax.dot_general(
        left, right, (((0,), (0,)), ((), ())), preferred_element_type=jnp.float32
    )


def key_positions(first, span_len, local_rows, half_dev, ctx_count, half_stretch, stretch_order):
    index_vec = first + lax.iota(jnp.int32, span_len)
    device_pos = index_vec // local_rows
    fsdp_pos = device_pos // ctx_count
    ctx_pos = device_pos % ctx_count
    row_pos = index_vec % local_rows
    halves = row_pos // half_dev
    within = row_pos % half_dev
    slot_match = ctx_pos[:, None] == lax.iota(jnp.int32, ctx_count)[None, :]
    paired = jnp.sum(jnp.where(slot_match, stretch_order[None, :], 0), axis=1)
    placed = jnp.where(halves == 0, paired, 2 * ctx_count - 1 - paired)
    return placed * half_stretch + fsdp_pos * half_dev + within


def key_block_len(span_len, local_rows):
    unit_count = span_len // local_rows
    upper_units = max(1, 2048 // local_rows)
    chosen = 1
    for divisor in range(1, min(unit_count, upper_units) + 1):
        if unit_count % divisor == 0:
            chosen = divisor
    return chosen * local_rows


def body_scores(query_five, key_blk, query_pos, query_seg, key_pos, key_seg):
    raw_scores = jnp.einsum(
        "sqkge,sbke->skgqb", query_five, key_blk, preferred_element_type=jnp.float32
    ) * HEAD_DIM ** (-0.5)
    capped = SOFT_CAP * jnp.tanh(raw_scores / SOFT_CAP)
    allowed = (query_seg[:, :, None] == key_seg[:, None, :]) & (
        key_pos[None, None, :] <= query_pos[None, :, None]
    )
    return (capped, allowed[:, None, None])


def on_device(
    tokens,
    segments,
    stretch_order,
    norm_gains,
    query_proj,
    keyval_proj,
    attn_proj,
    ffn_in,
    ffn_out,
    cotangent,
):
    f32 = jnp.float32
    bf16 = jnp.bfloat16
    seq_count = tokens.shape[0]
    half_dev = tokens.shape[3]
    model_width = tokens.shape[4]
    local_rows = 2 * half_dev
    row_count = seq_count * local_rows
    fsdp_count = lax.axis_size("fsdp")
    ctx_count = lax.axis_size("ctx")
    half_stretch = half_dev * fsdp_count
    gain_pre, gain_post, gain_ffn, gain_last = (
        norm_gains[0],
        norm_gains[1],
        norm_gains[2],
        norm_gains[3],
    )
    tok_in = tokens.reshape(row_count, model_width).astype(f32)
    seg_local = segments.reshape(seq_count, local_rows)
    own_first = (lax.axis_index("fsdp") * ctx_count + lax.axis_index("ctx")) * local_rows
    own_pos = key_positions(
        own_first, local_rows, local_rows, half_dev, ctx_count, half_stretch, stretch_order
    )
    xnorm = (tok_in * rms_factor(tok_in) * gain_pre).astype(bf16)
    full_query, full_keyval, full_attn = (
        lax.all_gather(query_proj, "fsdp", axis=0, tiled=True),
        lax.all_gather(keyval_proj, "fsdp", axis=0, tiled=True),
        lax.all_gather(attn_proj, "fsdp", axis=0, tiled=True),
    )
    qcols = full_query.shape[1]
    kcols = full_keyval.shape[2]
    kv_local = kcols // HEAD_DIM
    group = qcols // HEAD_DIM // kv_local
    keyval_flat_w = full_keyval.reshape(model_width, 2 * kcols)
    query = jnp.dot(xnorm, full_query, preferred_element_type=f32).astype(bf16)
    keyval = jnp.dot(xnorm, keyval_flat_w, preferred_element_type=f32).astype(bf16)
    query_five = query.reshape(seq_count, local_rows, kv_local, group, HEAD_DIM)
    keyval_four = keyval.reshape(seq_count, local_rows, 2, kcols)
    kv_first, seg_first = (
        lax.all_gather(keyval_four, ("fsdp", "ctx"), axis=1, tiled=True),
        lax.all_gather(seg_local, ("fsdp", "ctx"), axis=1, tiled=True),
    )
    fwd_total = kv_first.shape[1]
    fwd_len = key_block_len(fwd_total, local_rows)

    def fwd_step(step_index, partial_sums):
        denom, mixture = partial_sums
        offset = step_index * fwd_len
        kv_blk = lax.dynamic_slice_in_dim(kv_first, offset, fwd_len, 1)
        seg_blk = lax.dynamic_slice_in_dim(seg_first, offset, fwd_len, 1)
        pos_blk = key_positions(
            offset, fwd_len, local_rows, half_dev, ctx_count, half_stretch, stretch_order
        )
        keys_blk = kv_blk[:, :, 0].reshape(seq_count, fwd_len, kv_local, HEAD_DIM)
        vals_blk = kv_blk[:, :, 1].reshape(seq_count, fwd_len, kv_local, HEAD_DIM)
        capped, allowed = body_scores(query_five, keys_blk, own_pos, seg_local, pos_blk, seg_blk)
        expo = jnp.where(allowed, jnp.exp(capped), 0.0)
        denom = denom + jnp.sum(expo, axis=-1)
        mixture = mixture + jnp.einsum(
            "skgqb,sbke->sqkge", expo.astype(bf16), vals_blk, preferred_element_type=f32
        )
        return (denom, mixture)

    start_fold = (
        jnp.zeros((seq_count, kv_local, group, local_rows), f32),
        jnp.zeros((seq_count, local_rows, kv_local, group, HEAD_DIM), f32),
    )
    denom, mixture = lax.fori_loop(0, fwd_total // fwd_len, fwd_step, start_fold)
    attended_five = (mixture / jnp.transpose(denom, (0, 3, 1, 2))[..., None]).astype(bf16)
    lse_local = jnp.log(denom)
    attended = attended_five.reshape(row_count, qcols)
    branch = lax.psum(dot_nt(attended, full_attn), "tp")
    hidden = tok_in + branch * rms_factor(branch) * gain_post
    hnorm = (hidden * rms_factor(hidden) * gain_ffn).astype(bf16)
    full_in, full_out = (
        lax.all_gather(ffn_in, "fsdp", axis=0, tiled=True),
        lax.all_gather(ffn_out, "fsdp", axis=0, tiled=True),
    )
    ff_local = full_out.shape[1]
    both = jnp.dot(
        hnorm, full_in.reshape(model_width, 2 * ff_local), preferred_element_type=f32
    ).reshape(row_count, 2, ff_local)
    gelu_vals, gelu_slope = gelu_parts(both[:, 0])
    middle = (gelu_vals * both[:, 1]).astype(bf16)
    ffout = lax.psum(dot_nt(middle, full_out), "tp")
    result = (hidden + ffout * rms_factor(ffout) * gain_last).astype(bf16)
    cot_in = cotangent.reshape(row_count, model_width).astype(f32)
    grad_ff, grad_last_gain = norm_back(cot_in, ffout, gain_last)
    grad_ffb = grad_ff.astype(bf16)
    back_in, back_out = (
        lax.all_gather(ffn_in, "fsdp", axis=0, tiled=True),
        lax.all_gather(ffn_out, "fsdp", axis=0, tiled=True),
    )
    grad_mid = jnp.dot(grad_ffb, back_out, preferred_element_type=f32)
    grad_both = (
        jnp.stack([grad_mid * both[:, 1] * gelu_slope, grad_mid * gelu_vals], axis=1)
        .astype(bf16)
        .reshape(row_count, 2 * ff_local)
    )
    grad_hn = lax.psum(dot_nt(grad_both, back_in.reshape(model_width, 2 * ff_local)), "tp")
    grad_hid_n, grad_ffn_gain = norm_back(grad_hn, hidden, gain_ffn)
    grad_hidden = cot_in + grad_hid_n
    grad_branch, grad_post_gain = norm_back(grad_hidden, branch, gain_post)
    grad_branchb = grad_branch.astype(bf16)
    grad_attended = jnp.dot(grad_branchb, full_attn, preferred_element_type=f32).astype(bf16)
    grad_att_five = grad_attended.reshape(seq_count, local_rows, kv_local, group, HEAD_DIM)
    delta = jnp.einsum("sqkge,sqkge->skgq", grad_att_five.astype(f32), attended_five.astype(f32))
    kv_all, seg_all = (kv_first, seg_first)
    total_keys = kv_all.shape[1]
    back_len = key_block_len(total_keys, local_rows)

    def back_step(step_index, partial_sums):
        grad_q_acc, kv_term = partial_sums
        offset = step_index * back_len
        kv_blk = lax.dynamic_slice_in_dim(kv_all, offset, back_len, 1)
        seg_blk = lax.dynamic_slice_in_dim(seg_all, offset, back_len, 1)
        pos_blk = key_positions(
            offset, back_len, local_rows, half_dev, ctx_count, half_stretch, stretch_order
        )
        keys_blk = kv_blk[:, :, 0].reshape(seq_count, back_len, kv_local, HEAD_DIM)
        vals_blk = kv_blk[:, :, 1].reshape(seq_count, back_len, kv_local, HEAD_DIM)
        capped, allowed = body_scores(query_five, keys_blk, own_pos, seg_local, pos_blk, seg_blk)
        prob = jnp.where(allowed, jnp.exp(capped - lse_local[..., None]), 0.0)
        grad_prob = jnp.einsum(
            "sqkge,sbke->skgqb", grad_att_five, vals_blk, preferred_element_type=f32
        )
        ratio = capped / SOFT_CAP
        grad_raw = (
            prob * (grad_prob - delta[..., None]) * (1.0 - ratio * ratio) * HEAD_DIM ** (-0.5)
        )
        raw_half = grad_raw.astype(bf16)
        prob_half = prob.astype(bf16)
        grad_q_acc = grad_q_acc + jnp.einsum(
            "skgqb,sbke->sqkge", raw_half, keys_blk, preferred_element_type=f32
        )
        grad_keys = jnp.einsum(
            "skgqb,sqkge->sbke", raw_half, query_five, preferred_element_type=f32
        )
        grad_vals = jnp.einsum(
            "skgqb,sqkge->sbke", prob_half, grad_att_five, preferred_element_type=f32
        )
        block_term = jnp.stack(
            [
                grad_keys.reshape(seq_count, back_len, kcols),
                grad_vals.reshape(seq_count, back_len, kcols),
            ],
            axis=2,
        )
        kv_term = lax.dynamic_update_slice_in_dim(kv_term, block_term, offset, 1)
        return (grad_q_acc, kv_term)

    start_back = (
        jnp.zeros((seq_count, local_rows, kv_local, group, HEAD_DIM), f32),
        jnp.zeros((seq_count, total_keys, 2, kcols), f32),
    )
    grad_q_acc, kv_term = lax.fori_loop(0, total_keys // back_len, back_step, start_back)
    grad_kv_own = lax.psum_scatter(kv_term, ("fsdp", "ctx"), scatter_dimension=1, tiled=True)
    grad_kv_rows = grad_kv_own.astype(bf16).reshape(row_count, 2 * kcols)
    grad_q_rows = grad_q_acc.astype(bf16).reshape(row_count, qcols)
    grad_xnorm = lax.psum(
        (dot_nt(grad_q_rows, full_query) + dot_nt(grad_kv_rows, keyval_flat_w)).astype(
            jnp.bfloat16
        ),
        "tp",
    ).astype(jnp.float32)
    grad_x_n, grad_pre_gain = norm_back(grad_xnorm, tok_in, gain_pre)
    grad_tokens = (grad_hidden + grad_x_n).reshape(tokens.shape)
    gain_stack = jnp.stack([grad_pre_gain, grad_post_gain, grad_ffn_gain, grad_last_gain], axis=0)
    grad_gains = lax.psum(gain_stack, ("fsdp", "ctx"))
    right_attn_in = jnp.concatenate([grad_q_rows, grad_kv_rows], axis=1)
    pairs_list = (
        (xnorm, right_attn_in),
        (grad_branchb, attended),
        (hnorm, grad_both),
        (grad_ffb, middle),
    )
    columns_list = []
    for left_side, right_side in pairs_list:
        columns_list.append(dot_tn(left_side, right_side))
    summed = lax.psum_scatter(
        jnp.concatenate(columns_list, axis=1), "fsdp", scatter_dimension=0, tiled=True
    )
    summed = lax.psum(summed, "ctx")
    own_width = summed.shape[0]
    edge_two = qcols + 2 * kcols
    edge_three = edge_two + qcols
    edge_four = edge_three + 2 * ff_local
    grad_query = summed[:, :qcols]
    grad_keyval = summed[:, qcols:edge_two].reshape(own_width, 2, kcols)
    grad_attn = summed[:, edge_two:edge_three]
    grad_ffn_in = summed[:, edge_three:edge_four].reshape(own_width, 2, ff_local)
    grad_ffn_out = summed[:, edge_four:]
    return (
        result.reshape(tokens.shape),
        grad_tokens,
        grad_gains,
        grad_query,
        grad_keyval,
        grad_attn,
        grad_ffn_in,
        grad_ffn_out,
    )


def solution(mesh):
    placed = (
        P(None, None, "ctx", "fsdp", None),
        P(None, None, "ctx", "fsdp"),
        P(),
        P(),
        P("fsdp", "tp"),
        P("fsdp", None, "tp"),
        P("fsdp", "tp"),
        P("fsdp", None, "tp"),
        P("fsdp", "tp"),
        P(None, None, "ctx", "fsdp", None),
    )
    return jax.shard_map(
        on_device,
        mesh=mesh,
        in_specs=placed,
        out_specs=(
            P(None, None, "ctx", "fsdp", None),
            P(None, None, "ctx", "fsdp", None),
            P(),
            P("fsdp", "tp"),
            P("fsdp", None, "tp"),
            P("fsdp", "tp"),
            P("fsdp", None, "tp"),
            P("fsdp", "tp"),
        ),
        check_vma=False,
    )
```

profile of v0, /device:TPU:0, one launch (start us, length us, event | category | flops | bytes accessed | tf_op | source)
XLA Modules:
  0.0 3955.0 jit_solution(13872691908073583657)
XLA Ops:
  9.8 59.8 %all-gather.8.cloned.1.call-done = bf16[2304,2,512]{2,1,0:T(2,128)(2,1)} async-done(((bf16[576,2,512]{2,1,0:T(2,128)(2,1)}), bf16[2304,2,512]{2,1,0:T(2,128)(2,1)}) %all-gather.8.cloned.1.call-update) | async-done | bytes 4718608 | tf_op jit(solution)/shard_map/all_gather | solution.py:117
  69.7 3.8 copy.120
  79.6 39.7 %all-gather = s32[16,64,2]{1,2,0:T(2,128)S(1)} all-gather(s32[1,64,2]{1,2,0:T(2,128)S(1)} %bitcast.200), channel_id=1, replica_groups=mesh['fsdp'=4,'ctx'=4,'tp'=2] {'fsdp','ctx'}, dimensions={0}, use_global_device_ids=true | all-gather | bytes 8704 | tf_op jit(solution)/shard_map/all_gather | solution.py:131
  120.2 8.5 all-gather.12.cloned.1.call-done
  128.7 3.1 convolution_convert_fusion.2
  132.1 75.8 %all-gather.10.cloned.1.call-done = bf16[2,1024,2,512]{3,2,0,1:T(2,128)(2,1)} async-done(((bf16[2,64,2,512]{3,2,0,1:T(2,128)(2,1)}), bf16[2,1024,2,512]{3,2,0,1:T(2,128)(2,1)}) %all-gather.10.cloned.1.call-update) | async-done | bytes 4194320 | tf_op jit(solution)/shard_map/all_gather | solution.py:130
  207.8 10.0 fusion.86
  217.8 10.5 copy.119
  228.3 10.6 copy.118
  244.2 21.1 all-gather.14.cloned.1.call-done
  265.3 5.0 fusion.87
  270.4 10.2 copy.79
  281.6 8.6 all-reduce.6.cloned.1.call-done
  293.4 372.8 %all-gather.16.cloned.1.call-done = bf16[2304,2,4608]{2,0,1:T(8,128)(2,1)} async-done(((bf16[576,2,4608]{2,0,1:T(8,128)(2,1)}), bf16[2304,2,4608]{2,0,1:T(8,128)(2,1)}) %all-gather.16.cloned.1.call-update) | async-done | bytes 42467344 | tf_op jit(solution)/shard_map/all_gather | solution.py:166
  666.2 51.5 %copy.80 = bf16[2304,2,4608]{0,2,1:T(8,128)(2,1)} copy(bf16[2304,2,4608]{2,0,1:T(8,128)(2,1)} %all-gather.16.cloned.1.call-done) | data formatting | bytes 84934656 | tf_op jit(solution)/shard_map/all_gather | solution.py:166
  717.8 21.7 fusion
  739.5 3.2 multiply_convert_fusion
  742.6 121.0 %all-gather.18.cloned.1.call-done = bf16[2304,4608]{1,0:T(8,128)(2,1)} async-done(((bf16[576,4608]{1,0:T(8,128)(2,1)}), bf16[2304,4608]{1,0:T(8,128)(2,1)}) %all-gather.18.cloned.1.call-update) | async-done | bytes 21233680 | tf_op jit(solution)/shard_map/all_gather | solution.py:167
  863.6 12.0 fusion.88
  876.0 19.7 all-reduce.8.cloned.1.call-done
  902.1 12.5 fusion.10
  915.7 20.7 convolution_bitcast_fusion
  938.2 19.4 all-reduce.10.cloned.1.call-done
  963.9 3.2 convolution_convert_fusion.1
  968.0 4.6 fusion.42
  974.8 11.1 copy.88
  985.9 3.7 fusion.58
  989.6 10.9 copy.87
  1000.5 10.0 copy_bitcast_fusion
  1010.5 11.8 reshape.420
  1026.4 4.3 copy.89
  1030.7 16.6 fusion.91
  1047.4 31.6 fusion.84
  1081.6 5.2 fusion.90
  1086.7 119.2 %reduce-scatter.8.cloned.1.call-done = f32[64,2048]{1,0:T(8,128)} async-done(((f32[1024,2048]{1,0:T(8,128)}), f32[64,2048]{1,0:T(8,128)}) %reduce-scatter.8.cloned.1.call-update) | async-done | bytes 524304
  1207.3 8.3 fusion.52
  1215.6 99.1 %pad_maximum_fusion = f32[2304,16896]{1,0:T(8,128)} fusion(f32[2304,4608]{1,0:T(8,128)} %fusion.91, f32[2304,9216]{1,0:T(8,128)} %fusion.84, f32[2304,1024]{1,0:T(8,128)} %fusion.90, f32[2304,2048]{1,0:T(8,128)} %fusion.52), kind=kLoop, calls=%fused_computation | loop fusion | flops 116785152 | bytes 311427072 | tf_op jit(solution)/shard_map/concatenate | solution.py:271
  1315.0 4.0 fusion.89
  1319.0 5.0 fusion.2
  1324.1 1259.4 %reduce-scatter.6.cloned.1.call-done = f32[576,16896]{1,0:T(8,128)} async-done(((f32[2304,16896]{1,0:T(8,128)}), f32[576,16896]{1,0:T(8,128)}) %reduce-scatter.6.cloned.1.call-update) | async-done | bytes 38928400 | tf_op jit(solution)/shard_map/reduce_scatter | solution.py:270
  2584.2 20.9 all-reduce.12.cloned.1.call-done
  2606.6 87.2 %psum.46 = f32[4,2304]{1,0:T(4,128)} all-reduce(f32[4,2304]{1,0:T(4,128)S(1)} %pad_maximum_fusion.2), channel_id=1, replica_groups=mesh['fsdp'=4,'ctx'=4,'tp'=2] {'fsdp','ctx'}, use_global_device_ids=true, to_apply=%region_20.21 | all-reduce | flops 9216 | bytes 73728 | tf_op jit(solution)/shard_map/psum | solution.py:259
  2696.4 1192.0 %all-reduce.14.cloned.1.call-done = f32[576,16896]{1,0:T(8,128)} async-done(((f32[576,16896]{1,0:T(8,128)}), f32[576,16896]{1,0:T(8,128)}) %all-reduce.14.cloned.1.call-update) | async-done | bytes 38928400 | tf_op jit(solution)/shard_map/psum | solution.py:273
  3888.4 6.4 fusion.85
  3894.8 3.0 reshape.403
  3897.8 15.0 slice.66
  3912.8 26.6 reshape.404
  3939.4 8.9 slice.67
  (183 shorter events, 51.1 us)
Async XLA Ops:
  7.2 2.2 copy-start.2
  7.2 62.5 %all-gather.8.cloned.1.call-start = ((), (), s32[]{:S(2)}) async-start(), calls=%async_computation.2 | async-start | bytes 5898240 | tf_op jit(solution)/shard_map/all_gather | solution.py:117
  7.9 120.8 %all-gather.12.cloned.1.call-start = ((), (), s32[]{:S(2)}) async-start(), calls=%async_computation.4 | async-start | bytes 5898240 | tf_op jit(solution)/shard_map/all_gather | solution.py:116
  8.7 199.2 %all-gather.10.cloned.1.call-start = ((), (), s32[]{:S(2)}) async-start(), calls=%async_computation.3 | async-start | bytes 4456448 | tf_op jit(solution)/shard_map/all_gather | solution.py:130
  9.4 110.6 %copy-start.32 = (f32[2304]{0:T(1024)}, f32[2304]{0:T(1024)S(1)}, u32[]{:S(2)}) copy-start(f32[2304]{0:T(1024)S(1)} %get-tuple-element.119) | copy-start | bytes 27652
  9.4 282.3 %copy-start.34 = (f32[2304]{0:T(1024)}, f32[2304]{0:T(1024)S(1)}, u32[]{:S(2)}) copy-start(f32[2304]{0:T(1024)S(1)} %get-tuple-element.118) | copy-start | bytes 27652
  73.5 2.2 copy-start.1
  76.5 2.3 copy-start.46
  76.5 43.0 %copy-start.47 = (s32[4]{0:T(128)S(1)}, s32[4]{0:T(128)}, u32[]{:S(2)}) copy-start(s32[4]{0:T(128)} %param.12) | copy-start | bytes 52
  77.6 187.7 %all-gather.14.cloned.1.call-start = ((), (), s32[]{:S(2)}) async-start(), calls=%async_computation.5 | async-start | bytes 5898240 | tf_op jit(solution)/shard_map/all_gather | solution.py:118
  78.2 212.1 %all-reduce.6.cloned.1.call-start = ((), (), s32[]{:S(2)}) async-start(), calls=%async_computation.6 | async-start | bytes 2359296 | tf_op jit(solution)/shard_map/psum | solution.py:162
  78.3 53.5 %copy-start.41 = (f32[128]{0:T(128)}, f32[128]{0:T(128)S(1)}, u32[]{:S(2)}) copy-start(f32[128]{0:T(128)S(1)} %rsqrt.41) | copy-start | bytes 1540
  120.0 121.7 %copy-start.30 = (pred[2,64,1024]{2,1,0:T(8,128)(4,1)}, pred[2,64,1024]{2,1,0:T(8,128)(4,1)S(1)}, u32[]{:S(2)}) copy-start(pred[2,64,1024]{2,1,0:T(8,128)(4,1)S(1)} %compare_and_fusion) | copy-start | bytes 393220
  120.2 11.7 copy-start.11
  132.1 106.9 %copy-start.29 = (bf16[2,64,2,2,256]{4,3,2,1,0:T(2,128)(2,1)}, bf16[2,64,2,2,256]{4,3,2,1,0:T(2,128)(2,1)S(1)}, u32[]{:S(2)}) copy-start(bf16[2,64,2,2,256]{4,3,2,1,0:T(2,128)(2,1)S(1)} %reshape.393) | copy-start | bytes 786436
  238.9 2.8 copy-start.23
  244.2 26.1 copy-start.21
  270.3 395.9 %all-gather.16.cloned.1.call-start = ((), (), s32[]{:S(2)}) async-start(), calls=%async_computation.7 | async-start | bytes 53084160 | tf_op jit(solution)/shard_map/all_gather | solution.py:166
  280.6 583.0 %all-gather.18.cloned.1.call-start = ((), (), s32[]{:S(2)}) async-start(), calls=%async_computation.8 | async-start | bytes 26542080 | tf_op jit(solution)/shard_map/all_gather | solution.py:167
  281.4 614.3 %all-reduce.8.cloned.1.call-start = ((), (), s32[]{:S(2)}) async-start(), calls=%async_computation.9 | async-start | bytes 2359296 | tf_op jit(solution)/shard_map/psum | solution.py:175
  291.7 426.0 %copy-start.43 = (f32[128]{0:T(128)}, f32[128]{0:T(128)S(1)}, u32[]{:S(2)}) copy-start(f32[128]{0:T(128)S(1)} %add_rsqrt_fusion.3) | copy-start | bytes 1540
  875.7 81.9 %all-reduce.10.cloned.1.call-start = ((), (), s32[]{:S(2)}) async-start(), calls=%async_computation.10 | async-start | bytes 2359296 | tf_op jit(solution)/shard_map/psum | solution.py:190
  895.7 4.2 copy-start.7
  897.2 4.9 copy-start
  902.1 12.6 copy-start.18
  936.4 23.6 copy-start.4
  936.4 269.5 %reduce-scatter.8.cloned.1.call-start = ((), (), s32[]{:S(2)}) async-start(), calls=%async_computation.14 | async-start | bytes 8912896
  957.6 2.4 copy-start.13
  957.6 2.4 copy-start.14
  957.6 2.4 copy-start.35
  960.0 2.0 copy-start.44
  963.9 3.6 copy-start.28
  968.0 4.6 copy-start.24
  968.0 4.6 copy-start.26
  968.0 4.6 copy-start.40
  974.8 11.1 copy-start.17
  1022.3 1561.2 %reduce-scatter.6.cloned.1.call-start = ((), (), s32[]{:S(2)}) async-start(), calls=%async_computation.12 | async-start | bytes 194641920 | tf_op jit(solution)/shard_map/reduce_scatter | solution.py:270
  1026.4 4.3 copy-start.19
  1047.4 31.6 copy-start.8
  1078.9 2.6 copy-start.10
  1078.9 2.6 copy-start.22
  1086.7 120.6 %copy-start.12 = (bf16[128,2304]{1,0:T(8,128)(2,1)S(1)}, bf16[128,2304]{1,0:T(8,128)(2,1)}, u32[]{:S(2)}) copy-start(bf16[128,2304]{1,0:T(8,128)(2,1)} %copy-done.11) | copy-start | bytes 1769476
  1314.7 1290.3 %all-reduce.12.cloned.1.call-start = ((), (), s32[]{:S(2)}) async-start(), calls=%async_computation.11 | async-start | bytes 1179648 | tf_op jit(solution)/shard_map/psum | solution.py:250
  1324.0 2564.4 %all-reduce.14.cloned.1.call-start = ((), (), s32[]{:S(2)}) async-start(), calls=%async_computation.13 | async-start | bytes 77856768 | tf_op jit(solution)/shard_map/psum | solution.py:273
  2583.4 21.6 copy-start.3
  2583.4 21.6 copy-start.33
  2583.4 21.6 copy-start.42
  2583.5 110.4 %copy-start.6 = (f32[128,2304]{1,0:T(8,128)S(1)}, f32[128,2304]{1,0:T(8,128)}, u32[]{:S(2)}) copy-start(f32[128,2304]{1,0:T(8,128)} %copy-done.5) | copy-start | bytes 3538948
  (13 other events, 12.9 us)
Sparse Core Ops, SparseCore 0:
  9.9 59.7 all-gather.7
  71.5 57.1 all-gather.11
  132.1 75.7 all-gather.9
  209.5 55.6 all-gather.13
  270.4 19.7 all-reduce.5
  292.7 373.4 all-gather.15
  668.2 195.3 all-gather.17
  875.8 19.8 all-reduce.7
  936.5 20.9 all-reduce.9
  1022.4 183.4 reduce-scatter.7
  1314.8 1268.5 reduce-scatter.5
  2586.2 18.8 all-reduce.11
  2607.7 1280.6 all-reduce.13
where the time goes:
time: 3970 us; the launch traced here: 3960 us
  waiting for transfers between devices  3300 us (83%)
  local copies, waits for them, and re-layouts  209 us (5%)
  matrix products  166 us (4%)
  other arithmetic  136 us (3%)
  blocking collectives  127 us (3%)
    reduce_scatter x1, waiting for transfers between devices, on_device(): lax.psum_scatter(jnp.concatenate(columns_list, axis=1), 'fsdp', scatter_d...  1260 us
    psum x1, waiting for transfers between devices, on_device(): summed = lax.psum(summed, 'ctx')  1190 us
    all_gather x1, waiting for transfers between devices, on_device(): lax.all_gather(ffn_in, 'fsdp', axis=0, tiled=True)  373 us
    unnamed x14, waiting for transfers between devices  122 us
    all_gather x1, waiting for transfers between devices, on_device(): lax.all_gather(ffn_out, 'fsdp', axis=0, tiled=True)  121 us
    concatenate x1, other arithmetic, on_device(): jnp.concatenate(columns_list, axis=1)  99.1 us
    psum x1, blocking collectives, on_device(): grad_gains = lax.psum(gain_stack, ('fsdp', 'ctx'))  87.2 us
  transfers between devices with their start and end apart: 13, of which 13 were waited for; matrix products, arithmetic and copies ran while one was open for 5% of the time, Pallas kernels for 0%

commit v1 on v0

v1 whole, which is shorter than its diff:
```python
import jax
import jax.numpy as jnp
from jax import lax
from jax.sharding import PartitionSpec as P

HEAD_DIM = 256
SOFT_CAP = 50.0
NORM_EPS = 1e-06

F32 = jnp.float32
BF16 = jnp.bfloat16


def rms_factor(values):
    return lax.rsqrt(jnp.mean(values * values, axis=-1, keepdims=True) + NORM_EPS)


def norm_back(grad_out, values, scale_gain):
    factor = rms_factor(values)
    normed = values * factor
    grad_gain = jnp.sum(grad_out * normed, axis=0)
    scaled_grad = grad_out * scale_gain
    grad_in = factor * (
        scaled_grad - normed * jnp.mean(scaled_grad * normed, axis=-1, keepdims=True)
    )
    return (grad_in, grad_gain)


def gelu_parts(gate_vals):
    values, pullback = jax.vjp(lambda inputs: jax.nn.gelu(inputs, approximate=True), gate_vals)
    return (values, pullback(jnp.ones_like(gate_vals))[0])


def dot_nn(left, right):
    return jnp.dot(left, right, preferred_element_type=F32)


def dot_nt(left, right):
    return lax.dot_general(left, right, (((1,), (1,)), ((), ())), preferred_element_type=F32)


def dot_tn(left, right):
    return lax.dot_general(left, right, (((0,), (0,)), ((), ())), preferred_element_type=F32)


def swap(values, axis_name, offset):
    count = lax.axis_size(axis_name)
    return lax.ppermute(values, axis_name, [(i, i ^ offset) for i in range(count)])


def gather_xor(values, axis_name):
    count = lax.axis_size(axis_name)
    return jnp.stack([values] + [swap(values, axis_name, j) for j in range(1, count)])


def scatter_xor(parts, axis_name):
    total = parts[0].astype(F32)
    for j in range(1, lax.axis_size(axis_name)):
        total = total + swap(parts[j].astype(BF16), axis_name, j).astype(F32)
    return total


def gather_rows(rows):
    near = gather_xor(rows, "ctx").reshape(-1, rows.shape[-1])
    return gather_xor(near, "tp").reshape(-1, rows.shape[-1])


def scatter_rows(partial):
    width = partial.shape[-1]
    near = scatter_xor(partial.reshape(lax.axis_size("tp"), -1, width), "tp")
    return scatter_xor(near.reshape(lax.axis_size("ctx"), -1, width), "ctx")


def sum_all(values):
    for axis_name in ("tp", "ctx", "fsdp"):
        offset = 1
        while offset < lax.axis_size(axis_name):
            values = values + swap(values, axis_name, offset)
            offset *= 2
    return values


def xor_order(values, own_at, axis):
    offset = 1
    while offset < values.shape[axis]:
        halves = values.reshape(values.shape[:axis] + (-1, 2, offset) + values.shape[axis + 1 :])
        turned = jnp.flip(halves, axis + 1)
        if isinstance(own_at, int):
            picked = turned if own_at & offset else halves
        else:
            picked = jnp.where((own_at & offset) != 0, turned, halves)
        values = picked.reshape(values.shape)
        offset *= 2
    return values


def cols(values, start, width):
    return lax.dynamic_slice_in_dim(values, start, width, axis=values.ndim - 1)


def on_device(
    tokens,
    segments,
    stretch_order,
    norm_gains,
    query_proj,
    keyval_proj,
    attn_proj,
    ffn_in,
    ffn_out,
    cotangent,
):
    seq_count, _, _, half_dev, width = tokens.shape
    fsdp_count = lax.axis_size("fsdp")
    ctx_count = lax.axis_size("ctx")
    tp_count = lax.axis_size("tp")
    fsdp_at, ctx_at, tp_at = (lax.axis_index(name) for name in ("fsdp", "ctx", "tp"))
    row_count = seq_count * 2 * half_dev
    own_count = row_count // tp_count
    group_rows = own_count * tp_count * ctx_count
    assert seq_count == tp_count

    head_count = query_proj.shape[1] // HEAD_DIM
    group = head_count // (keyval_proj.shape[2] // HEAD_DIM)
    repeat = ctx_count // head_count
    assert repeat >= 1 and repeat * head_count == ctx_count
    sharers = group * repeat
    head_at = ctx_at // repeat
    kv_at = ctx_at // sharers
    share_at = ctx_at % sharers
    q_width = HEAD_DIM // repeat
    kv_width = 2 * HEAD_DIM // sharers
    q_own = (ctx_at % repeat) * q_width
    kv_own = share_at * kv_width
    ff_width = ffn_out.shape[1] // ctx_count
    ff_at = ctx_at * ff_width

    qkv_part = jnp.concatenate(
        [
            cols(query_proj, head_at * HEAD_DIM, HEAD_DIM),
            cols(keyval_proj[:, 0], kv_at * HEAD_DIM, HEAD_DIM),
            cols(keyval_proj[:, 1], kv_at * HEAD_DIM, HEAD_DIM),
        ],
        axis=1,
    )
    attn_part = cols(attn_proj, head_at * HEAD_DIM, HEAD_DIM)
    in_part = jnp.concatenate(
        [cols(ffn_in[:, 0], ff_at, ff_width), cols(ffn_in[:, 1], ff_at, ff_width)], axis=1
    )
    out_part = cols(ffn_out, ff_at, ff_width)
    w_qkv, w_attn, w_in, w_out = (
        lax.all_gather(part, "fsdp", axis=0, tiled=True)
        for part in (qkv_part, attn_part, in_part, out_part)
    )

    gain_pre, gain_post, gain_ffn, gain_last = (norm_gains[i] for i in range(4))
    row_at = tp_at * own_count
    tok_in = lax.dynamic_slice_in_dim(
        tokens.reshape(row_count, width), row_at, own_count, 0
    ).astype(F32)
    cot_in = lax.dynamic_slice_in_dim(
        cotangent.reshape(row_count, width), row_at, own_count, 0
    ).astype(F32)

    half_stretch = half_dev * fsdp_count
    seg_all = lax.all_gather(
        segments.reshape(seq_count, 2, half_dev), ("fsdp", "ctx"), axis=0, tiled=False
    ).reshape(fsdp_count, ctx_count, seq_count, 2, half_dev)
    ctx_ids = ctx_at ^ jnp.arange(ctx_count)
    fsdp_ids = fsdp_at ^ jnp.arange(fsdp_count)
    key_seg = xor_order(xor_order(xor_order(seg_all, fsdp_at, 0), ctx_at, 1), tp_at, 2)
    key_seg = key_seg.transpose(2, 0, 1, 3, 4)
    query_seg = key_seg[:, 0].reshape(seq_count, -1)
    key_seg = key_seg.reshape(seq_count, -1)
    paired = xor_order(stretch_order, ctx_at, 0)
    blocks = jnp.stack([paired, 2 * ctx_count - 1 - paired], axis=1)
    key_pos = (
        blocks[None, :, :, None] * half_stretch
        + fsdp_ids[:, None, None, None] * half_dev
        + jnp.arange(half_dev)[None, None, None, :]
    )
    query_pos = key_pos[0].reshape(-1)
    key_pos = key_pos.reshape(-1)
    allowed = (query_seg[:, :, None] == key_seg[:, None, :]) & (
        key_pos[None, None, :] <= query_pos[None, :, None]
    )

    xnorm_own = (tok_in * rms_factor(tok_in) * gain_pre).astype(BF16)
    xnorm = gather_rows(xnorm_own)
    qkv = dot_nn(xnorm, w_qkv).astype(BF16)
    query = qkv[:, :HEAD_DIM].reshape(seq_count, -1, HEAD_DIM)
    kv_own_rows = qkv[:, HEAD_DIM:].reshape(seq_count, -1, 2 * HEAD_DIM)
    kv_all = jnp.concatenate(
        [kv_own_rows] + [swap(kv_own_rows, "fsdp", j) for j in range(1, fsdp_count)], axis=1
    )
    keys, vals = kv_all[:, :, :HEAD_DIM], kv_all[:, :, HEAD_DIM:]
    raw_scores = jnp.einsum("sqe,ske->sqk", query, keys, preferred_element_type=F32)
    capped = SOFT_CAP * jnp.tanh(raw_scores * (HEAD_DIM ** (-0.5) / SOFT_CAP))
    expo = jnp.where(allowed, jnp.exp(capped), 0.0)
    denom = jnp.sum(expo, axis=-1, keepdims=True)
    mixture = jnp.einsum("sqk,ske->sqe", expo.astype(BF16), vals, preferred_element_type=F32)
    attended_seq = (mixture / denom).astype(BF16)
    lse = jnp.log(denom)
    attended = attended_seq.reshape(group_rows, HEAD_DIM)
    attended_own = attended if repeat == 1 else cols(attended, q_own, q_width)
    w_attn_own = w_attn if repeat == 1 else cols(w_attn, q_own, q_width)
    branch = scatter_rows(dot_nt(attended_own, w_attn_own))

    hidden = tok_in + branch * rms_factor(branch) * gain_post
    hnorm = gather_rows((hidden * rms_factor(hidden) * gain_ffn).astype(BF16))
    both = dot_nn(hnorm, w_in)
    gate, up = both[:, :ff_width], both[:, ff_width:]
    gelu_vals, gelu_slope = gelu_parts(gate)
    middle = (gelu_vals * up).astype(BF16)
    ffout = scatter_rows(dot_nt(middle, w_out))
    result = (hidden + ffout * rms_factor(ffout) * gain_last).astype(BF16)

    grad_ff, grad_last_gain = norm_back(cot_in, ffout, gain_last)
    grad_ffb = gather_rows(grad_ff.astype(BF16))
    grad_mid = dot_nn(grad_ffb, w_out)
    grad_both = jnp.concatenate(
        [grad_mid * up * gelu_slope, grad_mid * gelu_vals], axis=1
    ).astype(BF16)

    def weight_grad(left, right):
        return lax.psum_scatter(
            dot_tn(left, right).astype(BF16), "fsdp", scatter_dimension=0, tiled=True
        )

    def spread(part):
        return lax.all_gather(part, "ctx", axis=0, tiled=False)

    all_out = spread(weight_grad(grad_ffb, middle))
    all_in = spread(weight_grad(hnorm, grad_both))

    grad_hn = scatter_rows(dot_nt(grad_both, w_in))
    grad_hid_n, grad_ffn_gain = norm_back(grad_hn, hidden, gain_ffn)
    grad_hidden = cot_in + grad_hid_n
    grad_branch, grad_post_gain = norm_back(grad_hidden, branch, gain_post)
    grad_branchb = gather_rows(grad_branch.astype(BF16))

    grad_attended = dot_nn(grad_branchb, w_attn).astype(BF16)
    grad_att_seq = grad_attended.reshape(seq_count, -1, HEAD_DIM)
    delta = jnp.sum(
        grad_att_seq.astype(F32) * attended_seq.astype(F32), axis=-1, keepdims=True
    )
    prob = jnp.where(allowed, jnp.exp(capped - lse), 0.0)
    grad_prob = jnp.einsum("sqe,ske->sqk", grad_att_seq, vals, preferred_element_type=F32)
    ratio = capped / SOFT_CAP
    grad_raw = prob * (grad_prob - delta) * (1.0 - ratio * ratio) * HEAD_DIM ** (-0.5)
    raw_half = grad_raw.astype(BF16)
    prob_half = prob.astype(BF16)
    grad_q = jnp.einsum("sqk,ske->sqe", raw_half, keys, preferred_element_type=F32).astype(BF16)
    grad_k = jnp.einsum("sqk,sqe->ske", raw_half, query, preferred_element_type=F32)
    grad_v = jnp.einsum("sqk,sqe->ske", prob_half, grad_att_seq, preferred_element_type=F32)
    pieces = jnp.stack([grad_k, grad_v])
    pieces = pieces.reshape(2, *grad_k.shape[:2], sharers // 2, kv_width)
    pieces = pieces.transpose(0, 3, 1, 2, 4).reshape(sharers, *grad_k.shape[:2], kv_width)
    kv_term = lax.dynamic_index_in_dim(pieces, share_at, 0, keepdims=False)
    for j in range(repeat, sharers, repeat):
        sent = lax.dynamic_index_in_dim(pieces, share_at ^ j, 0, keepdims=False).astype(BF16)
        by_ctx = sent.reshape(seq_count, fsdp_count, ctx_count, -1, kv_width)
        sent = xor_order(by_ctx, j, 2).reshape(sent.shape)
        kv_term = kv_term + swap(sent, "ctx", j).astype(F32)
    kv_term = kv_term.reshape(seq_count, fsdp_count, -1, kv_width).transpose(1, 0, 2, 3)
    grad_kv = scatter_xor(kv_term, "fsdp").astype(BF16).reshape(group_rows, kv_width)
    grad_q = grad_q.reshape(group_rows, HEAD_DIM)
    grad_q_own = grad_q if repeat == 1 else cols(grad_q, q_own, q_width)
    grad_qkv = jnp.concatenate([grad_q_own, grad_kv], axis=1)
    w_q_own = w_qkv[:, :HEAD_DIM] if repeat == 1 else cols(w_qkv, q_own, q_width)
    w_qkv_own = jnp.concatenate([w_q_own, cols(w_qkv, HEAD_DIM + kv_own, kv_width)], axis=1)
    grad_xnorm = scatter_rows(dot_nt(grad_qkv, w_qkv_own))
    grad_x_n, grad_pre_gain = norm_back(grad_xnorm, tok_in, gain_pre)
    grad_tokens_own = grad_hidden + grad_x_n

    all_attn = spread(weight_grad(grad_branchb, attended_own))
    all_qkv = spread(weight_grad(xnorm, grad_qkv))

    own_width = all_out.shape[1]
    grad_gains = sum_all(
        jnp.stack([grad_pre_gain, grad_post_gain, grad_ffn_gain, grad_last_gain], axis=0)
    )
    result = lax.all_gather(result, "tp", axis=0, tiled=True)
    grad_tokens = lax.all_gather(grad_tokens_own, "tp", axis=0, tiled=True)

    def columns(spread_grad):
        return jnp.moveaxis(spread_grad, 0, -2).astype(F32)

    grad_query = columns(all_qkv[:, :, :q_width]).reshape(own_width, -1)
    grad_keyval = (
        all_qkv[:, :, q_width:]
        .reshape(ctx_count // sharers, 2, sharers // 2, own_width, kv_width)
        .transpose(3, 1, 0, 2, 4)
        .astype(F32)
        .reshape(own_width, 2, -1)
    )
    grad_attn = columns(all_attn).reshape(own_width, -1)
    grad_ffn_in = columns(all_in.reshape(ctx_count, own_width, 2, ff_width)).reshape(
        own_width, 2, -1
    )
    grad_ffn_out = columns(all_out).reshape(own_width, -1)
    return (
        result.reshape(tokens.shape),
        grad_tokens.reshape(tokens.shape),
        grad_gains,
        grad_query,
        grad_keyval,
        grad_attn,
        grad_ffn_in,
        grad_ffn_out,
    )


def solution(mesh):
    placed = (
        P(None, None, "ctx", "fsdp", None),
        P(None, None, "ctx", "fsdp"),
        P(),
        P(),
        P("fsdp", "tp"),
        P("fsdp", None, "tp"),
        P("fsdp", "tp"),
        P("fsdp", None, "tp"),
        P("fsdp", "tp"),
        P(None, None, "ctx", "fsdp", None),
    )
    return jax.shard_map(
        on_device,
        mesh=mesh,
        in_specs=placed,
        out_specs=(
            P(None, None, "ctx", "fsdp", None),
            P(None, None, "ctx", "fsdp", None),
            P(),
            P("fsdp", "tp"),
            P("fsdp", None, "tp"),
            P("fsdp", "tp"),
            P("fsdp", None, "tp"),
            P("fsdp", "tp"),
        ),
        check_vma=False,
    )
```

time: 3970 us -> 1140 us (0.29)
  waiting for transfers between devices: 3300 us -> 793 us
  other arithmetic: 136 us -> 30.8 us
  matrix products: 166 us -> 66.1 us
  local copies, waits for them, and re-layouts: 209 us -> 120 us
  blocking collectives: 127 us -> 55.4 us
  starting transfers between devices: 1.84 us -> 52.4 us
    psum x5 -> x0, waiting for transfers between devices: 1260 us -> none  [the longest x1 1190 us: on_device(): summed = lax.psum(summed, 'ctx')]
    reduce_scatter x1 -> x4, waiting for transfers between devices: 1260 us -> 154 us  [weight_grad(): lax.psum_scatter(dot_tn(left, right).astype(BF16), 'fsdp', scatter_dimens...]
    all_gather x6 -> x9, waiting for transfers between devices: 659 us -> 381 us  [the longest x4 340 us: spread(): return lax.all_gather(part, 'ctx', axis=0, tiled=False)]
    ppermute x0 -> x44, waiting for transfers between devices: none -> 257 us  [swap(): lax.ppermute(values, axis_name, [(i, i ^ offset) for i in range(count)])]
    unnamed x14 -> x13, waiting for transfers between devices: 122 us -> 1.34 us
    concatenate x1 -> x3, other arithmetic: 99.1 us -> 3.99 us  [the longest x1 1.69 us: on_device(): jnp.concatenate([cols(ffn_in[:, 0], ff_at, ff_width), cols(ffn_in[:, 1],...]
    psum x1 -> x0, blocking collectives: 87.2 us -> none  [on_device(): grad_gains = lax.psum(gain_stack, ('fsdp', 'ctx'))]
    ppermute x0 -> x44, starting transfers between devices: none -> 51.7 us  [swap(): lax.ppermute(values, axis_name, [(i, i ^ offset) for i in range(count)])]
  transfers between devices with their start and end apart: 13 -> 57, of which waited for: 13 -> 40; matrix products, arithmetic and copies ran while one was open for 5% -> 10% of each run, Pallas kernels for 0% -> 0%
where the time goes in v1:
time: 1140 us; the launch traced here: 1130 us
  waiting for transfers between devices  793 us (70%)
  local copies, waits for them, and re-layouts  120 us (11%)
  matrix products  66.1 us (6%)
  blocking collectives  55.4 us (5%)
  starting transfers between devices  52.4 us (5%)
  other arithmetic  30.8 us (3%)
  between operations  15.7 us (1%)
    all_gather x4, waiting for transfers between devices, spread(): return lax.all_gather(part, 'ctx', axis=0, tiled=False)  340 us
    ppermute x44, waiting for transfers between devices, swap(): lax.ppermute(values, axis_name, [(i, i ^ offset) for i in range(count)])  257 us
    reduce_scatter x4, waiting for transfers between devices, weight_grad(): lax.psum_scatter(dot_tn(left, right).astype(BF16), 'fsdp', scatter_dimens...  154 us
    all_gather x1, blocking collectives, on_device(): lax.all_gather(segments.reshape(seq_count, 2, half_dev), ('fsdp', 'ctx'),...  53.1 us
    ppermute x44, starting transfers between devices, swap(): lax.ppermute(values, axis_name, [(i, i ^ offset) for i in range(count)])  51.7 us
    all_gather x4, waiting for transfers between devices, on_device(): lax.all_gather(part, 'fsdp', axis=0, tiled=True)  41 us
    reshape x2, local copies, waits for them, and re-layouts, on_device(): columns(all_in.reshape(ctx_count, own_width, 2, ff_width))  38.1 us
  transfers between devices with their start and end apart: 57, of which 40 were waited for; matrix products, arithmetic and copies ran while one was open for 10% of the time, Pallas kernels for 0%

profile of v1, /device:TPU:0, one launch (start us, length us, event | category | flops | bytes accessed | tf_op | source)
XLA Modules:
  0.0 1134.2 jit_solution(17363637189309043584)
XLA Ops:
  7.2 3.8 fusion.96
  15.3 22.3 %fusion.89 = (bf16[576,1,4608]{2,1,0:T(2,128)(2,1)}, bf16[576,1,4608]{2,1,0:T(2,128)(2,1)}) fusion(bf16[576,2,4608]{2,1,0:T(2,128)(2,1)} %param.17), kind=kLoop, calls=%fused_computation.195 | loop fusion | bytes 21233664 | tf_op jit(solution)/shard_map/slice | solution.py:148
  37.6 8.0 constant_dynamic-slice_fusion.2
  49.8 5.1 collective-permute-start.2
  55.5 53.1 %all-gather = s32[32,2,1,32]{3,1,2,0:T(2,128)S(1)} all-gather(s32[2,2,1,32]{3,1,2,0:T(2,128)S(1)} %bitcast.246), channel_id=2, replica_groups=mesh['fsdp'=4,'ctx'=4,'tp'=2] {'fsdp','ctx'}, dimensions={0}, use_global_device_ids=true | all-gather | bytes 8704 | tf_op jit(solution)/shard_map/all_gather | solution.py:166
  113.6 4.7 convolution_convert_fusion.3
  122.7 22.6 %collective-permute-done.6 = bf16[2,256,512]{2,1,0:T(8,128)(2,1)S(1)} collective-permute-done((bf16[2,256,512]{2,1,0:T(8,128)(2,1)S(1)}, bf16[2,256,512]{2,1,0:T(8,128)(2,1)S(1)}, u32[]{:S(2)}, u32[]{:S(2)}) %collective-permute-start.6) | collective-permute-done | bytes 524320 | tf_op jit(solution)/shard_map/ppermute | solution.py:48
  145.3 10.2 collective-permute-done.5
  155.5 4.2 collective-permute-done.4
  175.3 3.6 collective-permute-start.10
  179.7 7.4 collective-permute-done.10
  187.1 17.3 %collective-permute-done.9 = bf16[64,2304]{1,0:T(8,128)(2,1)S(1)} collective-permute-done((bf16[64,2304]{1,0:T(8,128)(2,1)S(1)}, bf16[64,2304]{1,0:T(8,128)(2,1)S(1)}, u32[]{:S(2)}, u32[]{:S(2)}) %collective-permute-start.9) | collective-permute-done | bytes 294944 | tf_op jit(solution)/shard_map/ppermute | solution.py:48
  209.8 7.3 collective-permute-done.13
  217.1 14.3 %collective-permute-done.12 = bf16[64,2304]{1,0:T(8,128)(2,1)S(1)} collective-permute-done((bf16[64,2304]{1,0:T(8,128)(2,1)S(1)}, bf16[64,2304]{1,0:T(8,128)(2,1)S(1)}, u32[]{:S(2)}, u32[]{:S(2)}) %collective-permute-start.12) | collective-permute-done | bytes 294944 | tf_op jit(solution)/shard_map/ppermute | solution.py:48
  234.8 9.4 fusion.98
  248.2 41.0 %all-gather.21.cloned.1.call-done = bf16[2304,1152]{1,0:T(8,128)(2,1)} async-done(((bf16[576,1152]{1,0:T(8,128)(2,1)}), bf16[2304,1152]{1,0:T(8,128)(2,1)}) %all-gather.21.cloned.1.call-update) | async-done | bytes 5308432 | tf_op jit(solution)/shard_map/all_gather | solution.py:152
  289.2 6.1 fusion.99
  298.8 3.4 collective-permute-start.18
  303.2 7.4 collective-permute-done.18
  310.6 17.1 %collective-permute-done.17 = bf16[64,2304]{1,0:T(8,128)(2,1)S(1)} collective-permute-done((bf16[64,2304]{1,0:T(8,128)(2,1)S(1)}, bf16[64,2304]{1,0:T(8,128)(2,1)S(1)}, u32[]{:S(2)}, u32[]{:S(2)}) %collective-permute-start.17) | collective-permute-done | bytes 294944 | tf_op jit(solution)/shard_map/ppermute | solution.py:48
  334.3 7.5 collective-permute-done.21
  341.7 14.3 %collective-permute-done.20 = bf16[64,2304]{1,0:T(8,128)(2,1)S(1)} collective-permute-done((bf16[64,2304]{1,0:T(8,128)(2,1)S(1)}, bf16[64,2304]{1,0:T(8,128)(2,1)S(1)}, u32[]{:S(2)}, u32[]{:S(2)}) %collective-permute-start.20) | collective-permute-done | bytes 294944 | tf_op jit(solution)/shard_map/ppermute | solution.py:48
  359.4 4.3 fusion.8
  363.8 9.1 fusion.19
  377.9 2.9 collective-permute-start.24
  380.8 7.4 collective-permute-done.26
  388.2 14.3 %collective-permute-done.25 = bf16[64,2304]{1,0:T(8,128)(2,1)S(1)} collective-permute-done((bf16[64,2304]{1,0:T(8,128)(2,1)S(1)}, bf16[64,2304]{1,0:T(8,128)(2,1)S(1)}, u32[]{:S(2)}, u32[]{:S(2)}) %collective-permute-start.25) | collective-permute-done | bytes 294944 | tf_op jit(solution)/shard_map/ppermute | solution.py:48
  409.0 7.5 collective-permute-done.29
  416.4 14.4 %collective-permute-done.28 = bf16[64,2304]{1,0:T(8,128)(2,1)S(1)} collective-permute-done((bf16[64,2304]{1,0:T(8,128)(2,1)S(1)}, bf16[64,2304]{1,0:T(8,128)(2,1)S(1)}, u32[]{:S(2)}, u32[]{:S(2)}) %collective-permute-start.28) | collective-permute-done | bytes 294944 | tf_op jit(solution)/shard_map/ppermute | solution.py:48
  450.4 3.1 fusion
  453.6 22.3 %collective-permute-done.31 = bf16[2,1024,256]{2,1,0:T(8,128)(2,1)} collective-permute-done((bf16[2,1024,256]{2,1,0:T(8,128)(2,1)}, bf16[2,1024,256]{2,1,0:T(8,128)(2,1)}, u32[]{:S(2)}, u32[]{:S(2)}) %collective-permute-start.31) | collective-permute-done | bytes 1048608 | tf_op jit(solution)/shard_map/ppermute | solution.py:48
  481.7 6.2 collective-permute-done.34
  487.9 4.0 collective-permute-done.33
  497.3 5.0 convolution_convert_fusion.1
  504.3 9.8 convolution_convert_fusion
  525.4 7.4 collective-permute-done.38
  532.8 17.0 %collective-permute-done.37 = bf16[64,2304]{1,0:T(8,128)(2,1)S(1)} collective-permute-done((bf16[64,2304]{1,0:T(8,128)(2,1)S(1)}, bf16[64,2304]{1,0:T(8,128)(2,1)S(1)}, u32[]{:S(2)}, u32[]{:S(2)}) %collective-permute-start.37) | collective-permute-done | bytes 294944 | tf_op jit(solution)/shard_map/ppermute | solution.py:48
  552.6 45.3 %reduce-scatter.11.cloned.1.call-done = bf16[576,1152]{1,0:T(8,128)(2,1)} async-done(((bf16[2304,1152]{1,0:T(8,128)(2,1)}), bf16[576,1152]{1,0:T(8,128)(2,1)}) %reduce-scatter.11.cloned.1.call-update) | async-done | bytes 1327120 | tf_op jit(solution)/shard_map/reduce_scatter | solution.py:226
  598.0 108.2 %reduce-scatter.9.cloned.1.call-done = bf16[576,2304]{1,0:T(8,128)(2,1)} async-done(((bf16[2304,2304]{1,0:T(8,128)(2,1)}), bf16[576,2304]{1,0:T(8,128)(2,1)}) %reduce-scatter.9.cloned.1.call-update) | async-done | bytes 2654224 | tf_op jit(solution)/shard_map/reduce_scatter | solution.py:226
  725.4 25.3 %all-gather.27.cloned.1.call-done = bf16[2304,256]{1,0:T(8,128)(2,1)} async-done(((bf16[576,256]{1,0:T(8,128)(2,1)}), bf16[2304,256]{1,0:T(8,128)(2,1)}) %all-gather.27.cloned.1.call-update) | async-done | bytes 1179664 | tf_op jit(solution)/shard_map/all_gather | solution.py:231
  753.8 48.0 %all-gather.25.cloned.1.call-done = bf16[2304,512]{1,0:T(8,128)(2,1)} async-done(((bf16[576,512]{1,0:T(8,128)(2,1)}), bf16[2304,512]{1,0:T(8,128)(2,1)}) %all-gather.25.cloned.1.call-update) | async-done | bytes 2359312 | tf_op jit(solution)/shard_map/all_gather | solution.py:231
  806.7 4.0 reshape.367
  810.7 90.5 %all-gather.31.cloned.1.call-done = bf16[2304,1152]{1,0:T(8,128)(2,1)} async-done(((bf16[576,1152]{1,0:T(8,128)(2,1)}), bf16[2304,1152]{1,0:T(8,128)(2,1)}) %all-gather.31.cloned.1.call-update) | async-done | bytes 5308432 | tf_op jit(solution)/shard_map/all_gather | solution.py:231
  901.3 3.2 convert_bitcast_fusion
  904.5 6.4 copy.90
  910.9 176.4 %all-gather.29.cloned.1.call-done = bf16[2304,2304]{1,0:T(8,128)(2,1)} async-done(((bf16[576,2304]{1,0:T(8,128)(2,1)}), bf16[2304,2304]{1,0:T(8,128)(2,1)}) %all-gather.29.cloned.1.call-update) | async-done | bytes 10616848 | tf_op jit(solution)/shard_map/all_gather | solution.py:231
  1087.3 22.6 %reshape.382 = f32[4,576,2,1152]{3,2,1,0:T(2,128)} reshape(bf16[2304,2304]{1,0:T(8,128)(2,1)} %all-gather.29.cloned.1.call-done) | data formatting | bytes 31850496 | tf_op jit(solution)/shard_map/reshape | solution.py:298
  1109.9 15.5 %copy.89 = f32[4,576,1,2,1152]{4,3,0,2,1:T(2,128)} copy(f32[4,576,1,2,1152]{4,3,2,1,0:T(2,128)} %bitcast.164) | data formatting | bytes 42467328 | tf_op jit(solution)/shard_map/reshape | solution.py:298
  (355 shorter events, 147.9 us)
Async XLA Ops:
  7.2 106.4 %all-gather.15.cloned.1.call-start = ((), (), s32[]{:S(2)}) async-start(), calls=%async_computation.4 | async-start | bytes 4423680 | tf_op jit(solution)/shard_map/all_gather | solution.py:152
  13.5 150.9 %all-gather.17.cloned.1.call-start = ((), (), s32[]{:S(2)}) async-start(), calls=%async_computation.5 | async-start | bytes 1474560 | tf_op jit(solution)/shard_map/all_gather | solution.py:152
  15.3 219.5 %all-gather.19.cloned.1.call-start = ((), (), s32[]{:S(2)}) async-start(), calls=%async_computation.6 | async-start | bytes 13271040 | tf_op jit(solution)/shard_map/all_gather | solution.py:152
  47.8 241.5 %all-gather.21.cloned.1.call-start = ((), (), s32[]{:S(2)}) async-start(), calls=%async_computation.7 | async-start | bytes 6635520 | tf_op jit(solution)/shard_map/all_gather | solution.py:152
  49.8 59.1 %collective-permute-start.2 = (bf16[64,2304]{1,0:T(8,128)(2,1)S(1)}, bf16[64,2304]{1,0:T(8,128)(2,1)S(1)}, u32[]{:S(2)}, u32[]{:S(2)}) collective-permute-start(bf16[64,2304]{1,0:T(8,128)(2,1)S(1)} %fusion.49), channel_id=1, source_target_pairs={{0,6},{2,4},{4,2},{6,0},{1,7},{3,5},{5,3},{7,1},{8,14},{10,12},{12... | collective-permute-start | bytes 884744 | tf_op jit(solution)/shard_map/ppermute | solution.py:48
  54.9 54.0 %collective-permute-start.1 = (bf16[64,2304]{1,0:T(8,128)(2,1)S(1)}, bf16[64,2304]{1,0:T(8,128)(2,1)S(1)}, u32[]{:S(2)}, u32[]{:S(2)}) collective-permute-start(bf16[64,2304]{1,0:T(8,128)(2,1)S(1)} %fusion.49), channel_id=1, source_target_pairs={{0,4},{2,6},{4,0},{6,2},{1,5},{3,7},{5,1},{7,3},{8,12},{10,14},{12... | collective-permute-start | bytes 884744 | tf_op jit(solution)/shard_map/ppermute | solution.py:48
  54.9 54.0 %collective-permute-start = (bf16[64,2304]{1,0:T(8,128)(2,1)S(1)}, bf16[64,2304]{1,0:T(8,128)(2,1)S(1)}, u32[]{:S(2)}, u32[]{:S(2)}) collective-permute-start(bf16[64,2304]{1,0:T(8,128)(2,1)S(1)} %fusion.49), channel_id=1, source_target_pairs={{0,2},{2,0},{4,6},{6,4},{1,3},{3,1},{5,7},{7,5},{8,10},{10,8},{12,... | collective-permute-start | bytes 884744 | tf_op jit(solution)/shard_map/ppermute | solution.py:48
  118.3 27.0 %collective-permute-start.6 = (bf16[2,256,512]{2,1,0:T(8,128)(2,1)S(1)}, bf16[2,256,512]{2,1,0:T(8,128)(2,1)S(1)}, u32[]{:S(2)}, u32[]{:S(2)}) collective-permute-start(bf16[2,256,512]{2,1,0:T(8,128)(2,1)S(1)} %bitcast.202), channel_id=1, source_target_pairs={{0,24},{8,16},{16,8},{24,0},{1,25},{9,17},{17,9},{25,1},{2,26},{10... | collective-permute-start | bytes 1572872 | tf_op jit(solution)/shard_map/ppermute | solution.py:48
  118.4 37.1 %collective-permute-start.5 = (bf16[2,256,512]{2,1,0:T(8,128)(2,1)S(1)}, bf16[2,256,512]{2,1,0:T(8,128)(2,1)}, u32[]{:S(2)}, u32[]{:S(2)}) collective-permute-start(bf16[2,256,512]{2,1,0:T(8,128)(2,1)S(1)} %bitcast.203), channel_id=1, source_target_pairs={{0,16},{8,24},{16,0},{24,8},{1,17},{9,25},{17,1},{25,9},{2,18},{10... | collective-permute-start | bytes 1572872 | tf_op jit(solution)/shard_map/ppermute | solution.py:48
  120.1 39.6 %collective-permute-start.4 = (bf16[2,256,512]{2,1,0:T(8,128)(2,1)S(1)}, bf16[2,256,512]{2,1,0:T(8,128)(2,1)}, u32[]{:S(2)}, u32[]{:S(2)}) collective-permute-start(bf16[2,256,512]{2,1,0:T(8,128)(2,1)S(1)} %bitcast.204), channel_id=1, source_target_pairs={{0,8},{8,0},{16,24},{24,16},{1,9},{9,1},{17,25},{25,17},{2,10},{10... | collective-permute-start | bytes 1572872 | tf_op jit(solution)/shard_map/ppermute | solution.py:48
  172.8 378.4 %reduce-scatter.7.cloned.1.call-start = ((), (), s32[]{:S(2)}) async-start(), calls=%async_computation.10 | async-start | bytes 1474560 | tf_op jit(solution)/shard_map/reduce_scatter | solution.py:226
  175.3 11.9 %collective-permute-start.10 = (bf16[64,2304]{1,0:T(8,128)(2,1)S(1)}, bf16[64,2304]{1,0:T(8,128)(2,1)S(1)}, u32[]{:S(2)}, u32[]{:S(2)}) collective-permute-start(bf16[64,2304]{1,0:T(8,128)(2,1)S(1)} %get-tuple-element.79), channel_id=1, source_target_pairs={{0,6},{2,4},{4,2},{6,0},{1,7},{3,5},{5,3},{7,1},{8,14},{10,12},{12... | collective-permute-start | bytes 884744 | tf_op jit(solution)/shard_map/ppermute | solution.py:48
  178.8 25.6 %collective-permute-start.9 = (bf16[64,2304]{1,0:T(8,128)(2,1)S(1)}, bf16[64,2304]{1,0:T(8,128)(2,1)S(1)}, u32[]{:S(2)}, u32[]{:S(2)}) collective-permute-start(bf16[64,2304]{1,0:T(8,128)(2,1)S(1)} %get-tuple-element.80), channel_id=1, source_target_pairs={{0,4},{2,6},{4,0},{6,2},{1,5},{3,7},{5,1},{7,3},{8,12},{10,14},{12... | collective-permute-start | bytes 884744 | tf_op jit(solution)/shard_map/ppermute | solution.py:48
  178.9 25.6 %collective-permute-start.8 = (bf16[64,2304]{1,0:T(8,128)(2,1)S(1)}, bf16[64,2304]{1,0:T(8,128)(2,1)S(1)}, u32[]{:S(2)}, u32[]{:S(2)}) collective-permute-start(bf16[64,2304]{1,0:T(8,128)(2,1)S(1)} %get-tuple-element.78), channel_id=1, source_target_pairs={{0,2},{2,0},{4,6},{6,4},{1,3},{3,1},{5,7},{7,5},{8,10},{10,8},{12,... | collective-permute-start | bytes 884744 | tf_op jit(solution)/shard_map/ppermute | solution.py:48
  205.2 11.9 %collective-permute-start.13 = (bf16[64,2304]{1,0:T(8,128)(2,1)S(1)}, bf16[64,2304]{1,0:T(8,128)(2,1)S(1)}, u32[]{:S(2)}, u32[]{:S(2)}) collective-permute-start(bf16[64,2304]{1,0:T(8,128)(2,1)S(1)} %multiply_convert_fusion.4), channel_id=1, source_target_pairs={{0,6},{2,4},{4,2},{6,0},{1,7},{3,5},{5,3},{7,1},{8,14},{10,12},{12... | collective-permute-start | bytes 884744 | tf_op jit(solution)/shard_map/ppermute | solution.py:48
  207.6 23.8 %collective-permute-start.12 = (bf16[64,2304]{1,0:T(8,128)(2,1)S(1)}, bf16[64,2304]{1,0:T(8,128)(2,1)S(1)}, u32[]{:S(2)}, u32[]{:S(2)}) collective-permute-start(bf16[64,2304]{1,0:T(8,128)(2,1)S(1)} %multiply_convert_fusion.4), channel_id=1, source_target_pairs={{0,4},{2,6},{4,0},{6,2},{1,5},{3,7},{5,1},{7,3},{8,12},{10,14},{12... | collective-permute-start | bytes 884744 | tf_op jit(solution)/shard_map/ppermute | solution.py:48
  207.6 23.8 %collective-permute-start.11 = (bf16[64,2304]{1,0:T(8,128)(2,1)S(1)}, bf16[64,2304]{1,0:T(8,128)(2,1)S(1)}, u32[]{:S(2)}, u32[]{:S(2)}) collective-permute-start(bf16[64,2304]{1,0:T(8,128)(2,1)S(1)} %multiply_convert_fusion.4), channel_id=1, source_target_pairs={{0,2},{2,0},{4,6},{6,4},{1,3},{3,1},{5,7},{7,5},{8,10},{10,8},{12,... | collective-permute-start | bytes 884744 | tf_op jit(solution)/shard_map/ppermute | solution.py:48
  298.8 11.9 %collective-permute-start.18 = (bf16[64,2304]{1,0:T(8,128)(2,1)S(1)}, bf16[64,2304]{1,0:T(8,128)(2,1)S(1)}, u32[]{:S(2)}, u32[]{:S(2)}) collective-permute-start(bf16[64,2304]{1,0:T(8,128)(2,1)S(1)} %get-tuple-element.76), channel_id=1, source_target_pairs={{0,6},{2,4},{4,2},{6,0},{1,7},{3,5},{5,3},{7,1},{8,14},{10,12},{12... | collective-permute-start | bytes 884744 | tf_op jit(solution)/shard_map/ppermute | solution.py:48
  302.2 25.6 %collective-permute-start.17 = (bf16[64,2304]{1,0:T(8,128)(2,1)S(1)}, bf16[64,2304]{1,0:T(8,128)(2,1)S(1)}, u32[]{:S(2)}, u32[]{:S(2)}) collective-permute-start(bf16[64,2304]{1,0:T(8,128)(2,1)S(1)} %get-tuple-element.77), channel_id=1, source_target_pairs={{0,4},{2,6},{4,0},{6,2},{1,5},{3,7},{5,1},{7,3},{8,12},{10,14},{12... | collective-permute-start | bytes 884744 | tf_op jit(solution)/shard_map/ppermute | solution.py:48
  302.2 25.6 %collective-permute-start.16 = (bf16[64,2304]{1,0:T(8,128)(2,1)S(1)}, bf16[64,2304]{1,0:T(8,128)(2,1)S(1)}, u32[]{:S(2)}, u32[]{:S(2)}) collective-permute-start(bf16[64,2304]{1,0:T(8,128)(2,1)S(1)} %get-tuple-element.75), channel_id=1, source_target_pairs={{0,2},{2,0},{4,6},{6,4},{1,3},{3,1},{5,7},{7,5},{8,10},{10,8},{12,... | collective-permute-start | bytes 884744 | tf_op jit(solution)/shard_map/ppermute | solution.py:48
  329.9 11.8 %collective-permute-start.21 = (bf16[64,2304]{1,0:T(8,128)(2,1)S(1)}, bf16[64,2304]{1,0:T(8,128)(2,1)S(1)}, u32[]{:S(2)}, u32[]{:S(2)}) collective-permute-start(bf16[64,2304]{1,0:T(8,128)(2,1)S(1)} %get-tuple-element.86), channel_id=1, source_target_pairs={{0,6},{2,4},{4,2},{6,0},{1,7},{3,5},{5,3},{7,1},{8,14},{10,12},{12... | collective-permute-start | bytes 884744 | tf_op jit(solution)/shard_map/ppermute | solution.py:48
  332.3 23.8 %collective-permute-start.20 = (bf16[64,2304]{1,0:T(8,128)(2,1)S(1)}, bf16[64,2304]{1,0:T(8,128)(2,1)S(1)}, u32[]{:S(2)}, u32[]{:S(2)}) collective-permute-start(bf16[64,2304]{1,0:T(8,128)(2,1)S(1)} %get-tuple-element.86), channel_id=1, source_target_pairs={{0,4},{2,6},{4,0},{6,2},{1,5},{3,7},{5,1},{7,3},{8,12},{10,14},{12... | collective-permute-start | bytes 884744 | tf_op jit(solution)/shard_map/ppermute | solution.py:48
  332.3 23.8 %collective-permute-start.19 = (bf16[64,2304]{1,0:T(8,128)(2,1)S(1)}, bf16[64,2304]{1,0:T(8,128)(2,1)S(1)}, u32[]{:S(2)}, u32[]{:S(2)}) collective-permute-start(bf16[64,2304]{1,0:T(8,128)(2,1)S(1)} %get-tuple-element.86), channel_id=1, source_target_pairs={{0,2},{2,0},{4,6},{6,4},{1,3},{3,1},{5,7},{7,5},{8,10},{10,8},{12,... | collective-permute-start | bytes 884744 | tf_op jit(solution)/shard_map/ppermute | solution.py:48
  376.4 11.9 %collective-permute-start.26 = (bf16[64,2304]{1,0:T(8,128)(2,1)S(1)}, bf16[64,2304]{1,0:T(8,128)(2,1)S(1)}, u32[]{:S(2)}, u32[]{:S(2)}) collective-permute-start(bf16[64,2304]{1,0:T(8,128)(2,1)S(1)} %get-tuple-element.73), channel_id=1, source_target_pairs={{0,6},{2,4},{4,2},{6,0},{1,7},{3,5},{5,3},{7,1},{8,14},{10,12},{12... | collective-permute-start | bytes 884744 | tf_op jit(solution)/shard_map/ppermute | solution.py:48
  377.9 24.6 %collective-permute-start.25 = (bf16[64,2304]{1,0:T(8,128)(2,1)S(1)}, bf16[64,2304]{1,0:T(8,128)(2,1)S(1)}, u32[]{:S(2)}, u32[]{:S(2)}) collective-permute-start(bf16[64,2304]{1,0:T(8,128)(2,1)S(1)} %get-tuple-element.74), channel_id=1, source_target_pairs={{0,4},{2,6},{4,0},{6,2},{1,5},{3,7},{5,1},{7,3},{8,12},{10,14},{12... | collective-permute-start | bytes 884744 | tf_op jit(solution)/shard_map/ppermute | solution.py:48
  377.9 24.6 %collective-permute-start.24 = (bf16[64,2304]{1,0:T(8,128)(2,1)S(1)}, bf16[64,2304]{1,0:T(8,128)(2,1)S(1)}, u32[]{:S(2)}, u32[]{:S(2)}) collective-permute-start(bf16[64,2304]{1,0:T(8,128)(2,1)S(1)} %get-tuple-element.72), channel_id=1, source_target_pairs={{0,2},{2,0},{4,6},{6,4},{1,3},{3,1},{5,7},{7,5},{8,10},{10,8},{12,... | collective-permute-start | bytes 884744 | tf_op jit(solution)/shard_map/ppermute | solution.py:48
  404.5 11.9 %collective-permute-start.29 = (bf16[64,2304]{1,0:T(8,128)(2,1)S(1)}, bf16[64,2304]{1,0:T(8,128)(2,1)S(1)}, u32[]{:S(2)}, u32[]{:S(2)}) collective-permute-start(bf16[64,2304]{1,0:T(8,128)(2,1)S(1)} %multiply_convert_fusion.3), channel_id=1, source_target_pairs={{0,6},{2,4},{4,2},{6,0},{1,7},{3,5},{5,3},{7,1},{8,14},{10,12},{12... | collective-permute-start | bytes 884744 | tf_op jit(solution)/shard_map/ppermute | solution.py:48
  407.0 23.8 %collective-permute-start.28 = (bf16[64,2304]{1,0:T(8,128)(2,1)S(1)}, bf16[64,2304]{1,0:T(8,128)(2,1)S(1)}, u32[]{:S(2)}, u32[]{:S(2)}) collective-permute-start(bf16[64,2304]{1,0:T(8,128)(2,1)S(1)} %multiply_convert_fusion.3), channel_id=1, source_target_pairs={{0,4},{2,6},{4,0},{6,2},{1,5},{3,7},{5,1},{7,3},{8,12},{10,14},{12... | collective-permute-start | bytes 884744 | tf_op jit(solution)/shard_map/ppermute | solution.py:48
  407.0 23.8 %collective-permute-start.27 = (bf16[64,2304]{1,0:T(8,128)(2,1)S(1)}, bf16[64,2304]{1,0:T(8,128)(2,1)S(1)}, u32[]{:S(2)}, u32[]{:S(2)}) collective-permute-start(bf16[64,2304]{1,0:T(8,128)(2,1)S(1)} %multiply_convert_fusion.3), channel_id=1, source_target_pairs={{0,2},{2,0},{4,6},{6,4},{1,3},{3,1},{5,7},{7,5},{8,10},{10,8},{12,... | collective-permute-start | bytes 884744 | tf_op jit(solution)/shard_map/ppermute | solution.py:48
  450.4 25.5 %collective-permute-start.31 = (bf16[2,1024,256]{2,1,0:T(8,128)(2,1)}, bf16[2,1024,256]{2,1,0:T(8,128)(2,1)}, u32[]{:S(2)}, u32[]{:S(2)}) collective-permute-start(bf16[2,1024,256]{2,1,0:T(8,128)(2,1)} %bitcast.221), channel_id=1, source_target_pairs={{0,2},{2,0},{4,6},{6,4},{1,3},{3,1},{5,7},{7,5},{8,10},{10,8},{12,... | collective-permute-start | bytes 3145736 | tf_op jit(solution)/shard_map/ppermute | solution.py:48
  453.5 98.3 %reduce-scatter.5.cloned.1.call-start = ((), (), s32[]{:S(2)}) async-start(), calls=%async_computation.9 | async-start | bytes 2949120 | tf_op jit(solution)/shard_map/reduce_scatter | solution.py:226
  477.7 10.3 collective-permute-start.34
  479.2 12.7 %collective-permute-start.33 = (bf16[2,256,256]{2,1,0:T(8,128)(2,1)S(1)}, bf16[2,256,256]{2,1,0:T(8,128)(2,1)S(1)}, u32[]{:S(2)}, u32[]{:S(2)}) collective-permute-start(bf16[2,256,256]{2,1,0:T(8,128)(2,1)S(1)} %get-tuple-element.85), channel_id=1, source_target_pairs={{0,16},{8,24},{16,0},{24,8},{1,17},{9,25},{17,1},{25,9},{2,18},{10... | collective-permute-start | bytes 786440 | tf_op jit(solution)/shard_map/ppermute | solution.py:48
  480.7 11.3 collective-permute-start.32
  495.7 102.2 %reduce-scatter.11.cloned.1.call-start = ((), (), s32[]{:S(2)}) async-start(), calls=%async_computation.12 | async-start | bytes 6635520 | tf_op jit(solution)/shard_map/reduce_scatter | solution.py:226
  502.3 203.9 %reduce-scatter.9.cloned.1.call-start = ((), (), s32[]{:S(2)}) async-start(), calls=%async_computation.11 | async-start | bytes 13271040 | tf_op jit(solution)/shard_map/reduce_scatter | solution.py:226
  514.1 211.3 %all-gather.23.cloned.1.call-start = ((), (), s32[]{:S(2)}) async-start(), calls=%async_computation.8 | async-start | bytes 1769472 | tf_op jit(solution)/shard_map/all_gather | solution.py:284
  520.9 11.9 %collective-permute-start.38 = (bf16[64,2304]{1,0:T(8,128)(2,1)S(1)}, bf16[64,2304]{1,0:T(8,128)(2,1)S(1)}, u32[]{:S(2)}, u32[]{:S(2)}) collective-permute-start(bf16[64,2304]{1,0:T(8,128)(2,1)S(1)} %get-tuple-element.70), channel_id=1, source_target_pairs={{0,6},{2,4},{4,2},{6,0},{1,7},{3,5},{5,3},{7,1},{8,14},{10,12},{12... | collective-permute-start | bytes 884744 | tf_op jit(solution)/shard_map/ppermute | solution.py:48
  523.6 26.2 %collective-permute-start.37 = (bf16[64,2304]{1,0:T(8,128)(2,1)S(1)}, bf16[64,2304]{1,0:T(8,128)(2,1)S(1)}, u32[]{:S(2)}, u32[]{:S(2)}) collective-permute-start(bf16[64,2304]{1,0:T(8,128)(2,1)S(1)} %get-tuple-element.71), channel_id=1, source_target_pairs={{0,4},{2,6},{4,0},{6,2},{1,5},{3,7},{5,1},{7,3},{8,12},{10,14},{12... | collective-permute-start | bytes 884744 | tf_op jit(solution)/shard_map/ppermute | solution.py:48
  523.7 26.0 %collective-permute-start.36 = (bf16[64,2304]{1,0:T(8,128)(2,1)S(1)}, bf16[64,2304]{1,0:T(8,128)(2,1)S(1)}, u32[]{:S(2)}, u32[]{:S(2)}) collective-permute-start(bf16[64,2304]{1,0:T(8,128)(2,1)S(1)} %get-tuple-element.69), channel_id=1, source_target_pairs={{0,2},{2,0},{4,6},{6,4},{1,3},{3,1},{5,7},{7,5},{8,10},{10,8},{12,... | collective-permute-start | bytes 884744 | tf_op jit(solution)/shard_map/ppermute | solution.py:48
  551.2 199.5 %all-gather.27.cloned.1.call-start = ((), (), s32[]{:S(2)}) async-start(), calls=%async_computation.14 | async-start | bytes 1474560 | tf_op jit(solution)/shard_map/all_gather | solution.py:231
  551.8 250.1 %all-gather.25.cloned.1.call-start = ((), (), s32[]{:S(2)}) async-start(), calls=%async_computation.13 | async-start | bytes 2949120 | tf_op jit(solution)/shard_map/all_gather | solution.py:231
  552.5 348.7 %all-gather.31.cloned.1.call-start = ((), (), s32[]{:S(2)}) async-start(), calls=%async_computation.16 | async-start | bytes 6635520 | tf_op jit(solution)/shard_map/all_gather | solution.py:231
  597.9 489.4 %all-gather.29.cloned.1.call-start = ((), (), s32[]{:S(2)}) async-start(), calls=%async_computation.15 | async-start | bytes 13271040 | tf_op jit(solution)/shard_map/all_gather | solution.py:231
  707.7 4.0 collective-permute-start.40
  711.8 4.9 collective-permute-start.41
  716.7 4.0 collective-permute-start.42
  720.7 4.0 collective-permute-start.43
  (76 other events, 1765.3 us)
Sparse Core Ops, SparseCore 0:
  13.6 49.9 all-gather.14
  66.0 27.8 all-gather.16
  96.3 128.5 all-gather.18
  227.2 61.9 all-gather.20
  453.6 27.2 reduce-scatter.6
  495.8 36.4 reduce-scatter.4
  535.9 61.9 reduce-scatter.10
  601.6 104.5 reduce-scatter.8
  708.3 9.2 all-gather.22
  719.0 31.5 all-gather.26
  752.2 49.5 all-gather.24
  803.3 97.9 all-gather.30
  902.8 184.4 all-gather.28

commit v2 on v1

--- a/solution.py
+++ b/solution.py
@@ -50,25 +50,47 @@
 
 def gather_xor(values, axis_name):
     count = lax.axis_size(axis_name)
-    return jnp.stack([values] + [swap(values, axis_name, j) for j in range(1, count)])
+    held = {0: values}
+    offset = count // 2
+    while offset:
+        for j in tuple(held):
+            held[j ^ offset] = swap(held[j], axis_name, offset)
+        offset //= 2
+    return [held[j] for j in range(count)]
 
 
 def scatter_xor(parts, axis_name):
-    total = parts[0].astype(F32)
-    for j in range(1, lax.axis_size(axis_name)):
-        total = total + swap(parts[j].astype(BF16), axis_name, j).astype(F32)
-    return total
+    count = lax.axis_size(axis_name)
+    held = {j: parts[j] for j in range(count)}
+    offset = 1
+    while offset < count:
+        sent = [j for j in range(offset, count) if j & offset and j % offset == 0]
+        for j in reversed(sent):
+            got = swap(held.pop(j).astype(BF16), axis_name, offset)
+            held[j ^ offset] = held[j ^ offset].astype(F32) + got.astype(F32)
+        offset *= 2
+    return held[0]
 
 
 def gather_rows(rows):
-    near = gather_xor(rows, "ctx").reshape(-1, rows.shape[-1])
-    return gather_xor(near, "tp").reshape(-1, rows.shape[-1])
+    near = jnp.concatenate(gather_xor(rows, "ctx"), axis=0)
+    return jnp.concatenate(gather_xor(near, "tp"), axis=0)
 
 
 def scatter_rows(partial):
-    width = partial.shape[-1]
-    near = scatter_xor(partial.reshape(lax.axis_size("tp"), -1, width), "tp")
-    return scatter_xor(near.reshape(lax.axis_size("ctx"), -1, width), "ctx")
+    near = scatter_xor(jnp.split(partial, lax.axis_size("tp")), "tp")
+    return scatter_xor(jnp.split(near, lax.axis_size("ctx")), "ctx")
+
+
+def after(values, *others):
+    return lax.optimization_barrier((values, *others))[0]
+
+
+def both_cores(own, tp_at):
+    other = swap(own, "tp", 1)
+    first = jnp.where(tp_at == 0, own, other)
+    second = jnp.where(tp_at == 0, other, own)
+    return jnp.concatenate([first, second], axis=0)
 
 
 def sum_all(values):
@@ -135,23 +157,24 @@
     ff_width = ffn_out.shape[1] // ctx_count
     ff_at = ctx_at * ff_width
 
-    qkv_part = jnp.concatenate(
+    kv_part = cols(keyval_proj, kv_at * HEAD_DIM, HEAD_DIM)
+    att_part = jnp.concatenate(
         [
             cols(query_proj, head_at * HEAD_DIM, HEAD_DIM),
-            cols(keyval_proj[:, 0], kv_at * HEAD_DIM, HEAD_DIM),
-            cols(keyval_proj[:, 1], kv_at * HEAD_DIM, HEAD_DIM),
+            kv_part[:, 0],
+            kv_part[:, 1],
+            cols(attn_proj, head_at * HEAD_DIM, HEAD_DIM),
         ],
         axis=1,
     )
-    attn_part = cols(attn_proj, head_at * HEAD_DIM, HEAD_DIM)
-    in_part = jnp.concatenate(
-        [cols(ffn_in[:, 0], ff_at, ff_width), cols(ffn_in[:, 1], ff_at, ff_width)], axis=1
-    )
-    out_part = cols(ffn_out, ff_at, ff_width)
-    w_qkv, w_attn, w_in, w_out = (
-        lax.all_gather(part, "fsdp", axis=0, tiled=True)
-        for part in (qkv_part, attn_part, in_part, out_part)
-    )
+    w_att = lax.all_gather(att_part, "fsdp", axis=0, tiled=True)
+    w_qkv, w_attn = w_att[:, : 3 * HEAD_DIM], w_att[:, 3 * HEAD_DIM :]
+    in_part = cols(ffn_in, ff_at, ff_width)
+    ffn_part = jnp.concatenate(
+        [in_part[:, 0], in_part[:, 1], cols(ffn_out, ff_at, ff_width)], axis=1
+    )
+    w_ffn = lax.all_gather(ffn_part, "fsdp", axis=0, tiled=True)
+    w_in, w_out = w_ffn[:, : 2 * ff_width], w_ffn[:, 2 * ff_width :]
 
     gain_pre, gain_post, gain_ffn, gain_last = (norm_gains[i] for i in range(4))
     row_at = tp_at * own_count
@@ -163,26 +186,21 @@
     ).astype(F32)
 
     half_stretch = half_dev * fsdp_count
-    seg_all = lax.all_gather(
-        segments.reshape(seq_count, 2, half_dev), ("fsdp", "ctx"), axis=0, tiled=False
-    ).reshape(fsdp_count, ctx_count, seq_count, 2, half_dev)
-    ctx_ids = ctx_at ^ jnp.arange(ctx_count)
-    fsdp_ids = fsdp_at ^ jnp.arange(fsdp_count)
-    key_seg = xor_order(xor_order(xor_order(seg_all, fsdp_at, 0), ctx_at, 1), tp_at, 2)
-    key_seg = key_seg.transpose(2, 0, 1, 3, 4)
-    query_seg = key_seg[:, 0].reshape(seq_count, -1)
-    key_seg = key_seg.reshape(seq_count, -1)
-    paired = xor_order(stretch_order, ctx_at, 0)
-    blocks = jnp.stack([paired, 2 * ctx_count - 1 - paired], axis=1)
-    key_pos = (
-        blocks[None, :, :, None] * half_stretch
-        + fsdp_ids[:, None, None, None] * half_dev
-        + jnp.arange(half_dev)[None, None, None, :]
-    )
-    query_pos = key_pos[0].reshape(-1)
-    key_pos = key_pos.reshape(-1)
-    allowed = (query_seg[:, :, None] == key_seg[:, None, :]) & (
-        key_pos[None, None, :] <= query_pos[None, :, None]
+    length = 2 * ctx_count * half_stretch
+    slot = jnp.arange(ctx_count) == ctx_at
+    paired = jnp.sum(jnp.where(slot, stretch_order, 0))
+    block = jnp.stack([paired, 2 * ctx_count - 1 - paired])
+    position = block[:, None] * half_stretch + fsdp_at * half_dev + jnp.arange(half_dev)
+    marks = segments.reshape(seq_count, 2, half_dev) * length + position[None]
+    marks = marks.reshape(seq_count, 1, 2 * half_dev)
+    marks = jnp.concatenate(gather_xor(marks, "ctx"), axis=1).reshape(seq_count, 1, -1)
+    marks = jnp.concatenate(gather_xor(marks, "fsdp"), axis=1)
+    marks = jnp.where(tp_at == 0, marks, jnp.flip(marks, 0))
+    query_mark = marks[:, 0]
+    key_mark = marks.reshape(seq_count, -1)
+    query_first = query_mark - lax.rem(query_mark, length)
+    allowed = (key_mark[:, None, :] <= query_mark[:, :, None]) & (
+        key_mark[:, None, :] >= query_first[:, :, None]
     )
 
     xnorm_own = (tok_in * rms_factor(tok_in) * gain_pre).astype(BF16)
@@ -190,9 +208,7 @@
     qkv = dot_nn(xnorm, w_qkv).astype(BF16)
     query = qkv[:, :HEAD_DIM].reshape(seq_count, -1, HEAD_DIM)
     kv_own_rows = qkv[:, HEAD_DIM:].reshape(seq_count, -1, 2 * HEAD_DIM)
-    kv_all = jnp.concatenate(
-        [kv_own_rows] + [swap(kv_own_rows, "fsdp", j) for j in range(1, fsdp_count)], axis=1
-    )
+    kv_all = jnp.concatenate(gather_xor(kv_own_rows, "fsdp"), axis=1)
     keys, vals = kv_all[:, :, :HEAD_DIM], kv_all[:, :, HEAD_DIM:]
     raw_scores = jnp.einsum("sqe,ske->sqk", query, keys, preferred_element_type=F32)
     capped = SOFT_CAP * jnp.tanh(raw_scores * (HEAD_DIM ** (-0.5) / SOFT_CAP))
@@ -230,14 +246,16 @@
     def spread(part):
         return lax.all_gather(part, "ctx", axis=0, tiled=False)
 
-    all_out = spread(weight_grad(grad_ffb, middle))
-    all_in = spread(weight_grad(hnorm, grad_both))
+    part_out = weight_grad(grad_ffb, middle)
+    part_in = weight_grad(hnorm, grad_both)
 
     grad_hn = scatter_rows(dot_nt(grad_both, w_in))
     grad_hid_n, grad_ffn_gain = norm_back(grad_hn, hidden, gain_ffn)
     grad_hidden = cot_in + grad_hid_n
     grad_branch, grad_post_gain = norm_back(grad_hidden, branch, gain_post)
     grad_branchb = gather_rows(grad_branch.astype(BF16))
+    grad_branchb = after(grad_branchb, part_out)
+    all_out = spread(part_out)
 
     grad_attended = dot_nn(grad_branchb, w_attn).astype(BF16)
     grad_att_seq = grad_attended.reshape(seq_count, -1, HEAD_DIM)
@@ -262,26 +280,34 @@
         by_ctx = sent.reshape(seq_count, fsdp_count, ctx_count, -1, kv_width)
         sent = xor_order(by_ctx, j, 2).reshape(sent.shape)
         kv_term = kv_term + swap(sent, "ctx", j).astype(F32)
-    kv_term = kv_term.reshape(seq_count, fsdp_count, -1, kv_width).transpose(1, 0, 2, 3)
-    grad_kv = scatter_xor(kv_term, "fsdp").astype(BF16).reshape(group_rows, kv_width)
+    kv_term = kv_term.reshape(seq_count, fsdp_count, -1, kv_width)
+    grad_kv = scatter_xor([kv_term[:, j] for j in range(fsdp_count)], "fsdp").astype(BF16).reshape(group_rows, kv_width)
     grad_q = grad_q.reshape(group_rows, HEAD_DIM)
     grad_q_own = grad_q if repeat == 1 else cols(grad_q, q_own, q_width)
     grad_qkv = jnp.concatenate([grad_q_own, grad_kv], axis=1)
+    grad_qkv = after(grad_qkv, part_in)
+    own_width = part_in.shape[0]
+    part_in = jnp.stack([part_in[:, :ff_width], part_in[:, ff_width:]], axis=1)
+    all_in = spread(part_in)
     w_q_own = w_qkv[:, :HEAD_DIM] if repeat == 1 else cols(w_qkv, q_own, q_width)
     w_qkv_own = jnp.concatenate([w_q_own, cols(w_qkv, HEAD_DIM + kv_own, kv_width)], axis=1)
     grad_xnorm = scatter_rows(dot_nt(grad_qkv, w_qkv_own))
     grad_x_n, grad_pre_gain = norm_back(grad_xnorm, tok_in, gain_pre)
     grad_tokens_own = grad_hidden + grad_x_n
 
-    all_attn = spread(weight_grad(grad_branchb, attended_own))
-    all_qkv = spread(weight_grad(xnorm, grad_qkv))
-
-    own_width = all_out.shape[1]
+    att_term = jnp.concatenate(
+        [dot_tn(xnorm, grad_qkv).astype(BF16), dot_tn(grad_branchb, attended_own).astype(BF16)],
+        axis=1,
+    )
+    att_term = after(att_term, all_out)
+    all_att = spread(lax.psum_scatter(att_term, "fsdp", scatter_dimension=0, tiled=True))
+    all_qkv, all_attn = all_att[:, :, : q_width + kv_width], all_att[:, :, q_width + kv_width :]
+
     grad_gains = sum_all(
         jnp.stack([grad_pre_gain, grad_post_gain, grad_ffn_gain, grad_last_gain], axis=0)
     )
-    result = lax.all_gather(result, "tp", axis=0, tiled=True)
-    grad_tokens = lax.all_gather(grad_tokens_own, "tp", axis=0, tiled=True)
+    result = both_cores(result, tp_at)
+    grad_tokens = both_cores(grad_tokens_own, tp_at)
 
     def columns(spread_grad):
         return jnp.moveaxis(spread_grad, 0, -2).astype(F32)
@@ -295,9 +321,7 @@
         .reshape(own_width, 2, -1)
     )
     grad_attn = columns(all_attn).reshape(own_width, -1)
-    grad_ffn_in = columns(all_in.reshape(ctx_count, own_width, 2, ff_width)).reshape(
-        own_width, 2, -1
-    )
+    grad_ffn_in = columns(all_in).reshape(own_width, 2, -1)
     grad_ffn_out = columns(all_out).reshape(own_width, -1)
     return (
         result.reshape(tokens.shape),

time: 1140 us -> 1000 us (0.88)
  waiting for transfers between devices: 793 us -> 690 us
  blocking collectives: 55.4 us -> 0 us
  starting transfers between devices: 52.4 us -> 75.4 us
    reduce_scatter x4 -> x2, waiting for transfers between devices: 154 us -> 26.8 us  [weight_grad(): lax.psum_scatter(dot_tn(left, right).astype(BF16), 'fsdp', scatter_dimens...]
    all_gather x4 -> x3, waiting for transfers between devices: 340 us -> 258 us  [spread(): return lax.all_gather(part, 'ctx', axis=0, tiled=False)]
    ppermute x44 -> x52, waiting for transfers between devices: 257 us -> 316 us  [swap(): lax.ppermute(values, axis_name, [(i, i ^ offset) for i in range(count)])]
    all_gather x2 -> x0, blocking collectives: 55.4 us -> none  [the longest x1 53.1 us: on_device(): lax.all_gather(segments.reshape(seq_count, 2, half_dev), ('fsdp', 'ctx'),...]
    reduce_scatter x0 -> x1, waiting for transfers between devices: none -> 45.7 us  [on_device(): lax.psum_scatter(att_term, 'fsdp', scatter_dimension=0, tiled=True)]
    slice x12 -> x4, local copies, waits for them, and re-layouts: 27.9 us -> 13.7 us  [the longest x1 8.93 us: on_device(): in_part[:, 0]]
    ppermute x44 -> x52, starting transfers between devices: 51.7 us -> 63.6 us  [swap(): lax.ppermute(values, axis_name, [(i, i ^ offset) for i in range(count)])]
    unnamed x140 -> x90, local copies, waits for them, and re-layouts: 15.4 us -> 23.8 us
  transfers between devices with their start and end apart: 57 -> 60, of which waited for: 40 -> 45; matrix products, arithmetic and copies ran while one was open for 10% -> 11% of each run, Pallas kernels for 0% -> 0%
where the time goes in v2:
time: 1000 us; the launch traced here: 993 us
  waiting for transfers between devices  690 us (69%)
  local copies, waits for them, and re-layouts  114 us (11%)
  starting transfers between devices  75.4 us (8%)
  matrix products  66.5 us (7%)
  other arithmetic  31.2 us (3%)
  between operations  16 us (2%)
    ppermute x52, waiting for transfers between devices, swap(): lax.ppermute(values, axis_name, [(i, i ^ offset) for i in range(count)])  316 us
    all_gather x3, waiting for transfers between devices, spread(): return lax.all_gather(part, 'ctx', axis=0, tiled=False)  258 us
    ppermute x52, starting transfers between devices, swap(): lax.ppermute(values, axis_name, [(i, i ^ offset) for i in range(count)])  63.6 us
    reshape x2, local copies, waits for them, and re-layouts, on_device(): grad_ffn_in = columns(all_in).reshape(own_width, 2, -1)  51.7 us
    reduce_scatter x1, waiting for transfers between devices, on_device(): lax.psum_scatter(att_term, 'fsdp', scatter_dimension=0, tiled=True)  45.7 us
    all_gather x1, waiting for transfers between devices, on_device(): w_ffn = lax.all_gather(ffn_part, 'fsdp', axis=0, tiled=True)  43.6 us
    reduce_scatter x2, waiting for transfers between devices, weight_grad(): lax.psum_scatter(dot_tn(left, right).astype(BF16), 'fsdp', scatter_dimens...  26.8 us
    dot_general x4, matrix products, dot_nn(): return jnp.dot(left, right, preferred_element_type=F32)  25.6 us
  transfers between devices with their start and end apart: 60, of which 45 were waited for; matrix products, arithmetic and copies ran while one was open for 11% of the time, Pallas kernels for 0%

profile of v2, /device:TPU:0, one launch (start us, length us, event | category | flops | bytes accessed | tf_op | source)
XLA Modules:
  0.0 993.1 jit_solution(16721441436046382293)
XLA Ops:
  13.9 8.9 constant_dynamic-slice_fusion
  25.4 10.8 %reduce-scatter.6.cloned.1.call-start = ((), (), s32[]{:S(2)}) async-start(), calls=%async_computation.5 | async-start | bytes 6635520 | tf_op jit(solution)/shard_map/reduce_scatter | solution.py:242
  37.4 4.1 collective-permute-start.7
  43.0 11.9 %collective-permute-done.7 = bf16[64,2304]{1,0:T(8,128)(2,1)S(1)} collective-permute-done((bf16[64,2304]{1,0:T(8,128)(2,1)S(1)}, bf16[64,2304]{1,0:T(8,128)(2,1)S(1)}, u32[]{:S(2)}, u32[]{:S(2)}) %collective-permute-start.7) | collective-permute-done | bytes 294944 | tf_op jit(solution)/shard_map/ppermute | solution.py:48
  57.9 5.1 collective-permute-done.8
  74.2 4.7 convolution_convert_fusion.4
  82.6 14.3 %collective-permute-done.4 = s32[2,1,256]{2,0,1:T(2,128)S(1)} collective-permute-done((s32[2,1,256]{2,0,1:T(2,128)S(1)}, s32[2,1,256]{2,0,1:T(2,128)S(1)}, u32[]{:S(2)}, u32[]{:S(2)}) %collective-permute-start.4) | collective-permute-done | bytes 2080 | tf_op jit(solution)/shard_map/ppermute | solution.py:48
  102.8 23.9 %collective-permute-done.10 = bf16[2,256,512]{2,1,0:T(8,128)(2,1)S(1)} collective-permute-done((bf16[2,256,512]{2,1,0:T(8,128)(2,1)S(1)}, bf16[2,256,512]{2,1,0:T(8,128)(2,1)S(1)}, u32[]{:S(2)}, u32[]{:S(2)}) %collective-permute-start.10) | collective-permute-done | bytes 524320 | tf_op jit(solution)/shard_map/ppermute | solution.py:48
  126.7 20.2 %collective-permute-done.12 = bf16[2,256,512]{2,1,0:T(8,128)(2,1)S(1)} collective-permute-done((bf16[2,256,512]{2,1,0:T(8,128)(2,1)S(1)}, bf16[2,256,512]{2,1,0:T(8,128)(2,1)S(1)}, u32[]{:S(2)}, u32[]{:S(2)}) %collective-permute-start.12) | collective-permute-done | bytes 524320 | tf_op jit(solution)/shard_map/ppermute | solution.py:48
  157.2 7.8 collective-permute-done.15
  167.8 8.1 collective-permute-done.14
  175.9 4.1 collective-permute-done.16
  184.6 8.4 collective-permute-done.18
  193.1 6.6 collective-permute-done.19
  203.8 43.6 %all-gather.11.cloned.1.call-done = bf16[2304,3456]{1,0:T(8,128)(2,1)} async-done(((bf16[576,3456]{1,0:T(8,128)(2,1)}), bf16[2304,3456]{1,0:T(8,128)(2,1)}) %all-gather.11.cloned.1.call-update) | async-done | bytes 15925264 | tf_op jit(solution)/shard_map/all_gather | solution.py:176
  247.4 8.8 fusion.2
  258.4 5.7 fusion.6
  269.6 7.8 collective-permute-done.23
  279.9 8.3 collective-permute-done.22
  288.2 4.0 collective-permute-done.24
  298.2 8.4 collective-permute-done.27
  307.3 6.9 collective-permute-done.28
  318.7 5.0 convolution_convert_fusion.1
  324.0 8.9 fusion.15
  334.3 9.8 convolution_convert_fusion
  344.2 9.3 fusion
  358.9 7.8 collective-permute-done.32
  370.1 7.7 collective-permute-done.31
  377.8 4.4 collective-permute-done.33
  392.4 12.2 %collective-permute-done.35 = bf16[64,2304]{1,0:T(8,128)(2,1)S(1)} collective-permute-done((bf16[64,2304]{1,0:T(8,128)(2,1)S(1)}, bf16[64,2304]{1,0:T(8,128)(2,1)S(1)}, u32[]{:S(2)}, u32[]{:S(2)}) %collective-permute-start.35) | collective-permute-done | bytes 294944 | tf_op jit(solution)/shard_map/ppermute | solution.py:48
  405.0 7.5 collective-permute-done.36
  429.0 23.8 %collective-permute-done.38 = bf16[2,1024,256]{2,1,0:T(8,128)(2,1)S(1)} collective-permute-done((bf16[2,1024,256]{2,1,0:T(8,128)(2,1)}, bf16[2,1024,256]{2,1,0:T(8,128)(2,1)S(1)}, u32[]{:S(2)}, u32[]{:S(2)}) %collective-permute-start.38) | collective-permute-done | bytes 1048608 | tf_op jit(solution)/shard_map/ppermute | solution.py:48
  457.2 5.4 collective-permute-done.40
  464.5 5.7 collective-permute-done.39
  470.2 5.4 collective-permute-done.41
  475.7 23.7 %reduce-scatter.8.cloned.1.call-done = bf16[576,2304]{1,0:T(8,128)(2,1)} async-done(((bf16[2304,2304]{1,0:T(8,128)(2,1)}), bf16[576,2304]{1,0:T(8,128)(2,1)}) %reduce-scatter.8.cloned.1.call-update) | async-done | bytes 2654224 | tf_op jit(solution)/shard_map/reduce_scatter | solution.py:242
  501.1 99.9 %all-gather.13.cloned.1.call-done = bf16[2304,1152]{1,0:T(8,128)(2,1)} async-done(((bf16[576,1152]{1,0:T(8,128)(2,1)}), bf16[2304,1152]{1,0:T(8,128)(2,1)}) %all-gather.13.cloned.1.call-update) | async-done | bytes 5308432 | tf_op jit(solution)/shard_map/all_gather | solution.py:247
  604.7 45.7 %reduce-scatter.10.cloned.1.call-done = bf16[576,768]{1,0:T(8,128)(2,1)} async-done(((bf16[2304,768]{1,0:T(8,128)(2,1)}), bf16[576,768]{1,0:T(8,128)(2,1)}) %reduce-scatter.10.cloned.1.call-update) | async-done | bytes 884752 | tf_op jit(solution)/shard_map/reduce_scatter | solution.py:303
  663.0 28.0 %collective-permute-done.44 = bf16[64,2304]{1,0:T(8,128)(2,1)S(1)} collective-permute-done((bf16[64,2304]{1,0:T(8,128)(2,1)S(1)}, bf16[64,2304]{1,0:T(8,128)(2,1)S(1)}, u32[]{:S(2)}, u32[]{:S(2)}) %collective-permute-start.44) | collective-permute-done | bytes 294944 | tf_op jit(solution)/shard_map/ppermute | solution.py:48
  692.7 15.4 %collective-permute-done.43 = bf16[64,2304]{1,0:T(8,128)(2,1)S(1)} collective-permute-done((bf16[64,2304]{1,0:T(8,128)(2,1)S(1)}, bf16[64,2304]{1,0:T(8,128)(2,1)S(1)}, u32[]{:S(2)}, u32[]{:S(2)}) %collective-permute-start.43) | collective-permute-done | bytes 294944 | tf_op jit(solution)/shard_map/ppermute | solution.py:48
  708.1 17.7 %collective-permute-done.45 = bf16[64,2304]{1,0:T(8,128)(2,1)S(1)} collective-permute-done((bf16[64,2304]{1,0:T(8,128)(2,1)S(1)}, bf16[64,2304]{1,0:T(8,128)(2,1)S(1)}, u32[]{:S(2)}, u32[]{:S(2)}) %collective-permute-start.45) | collective-permute-done | bytes 294944 | tf_op jit(solution)/shard_map/ppermute | solution.py:48
  736.8 4.5 collective-permute-done.49
  747.5 6.6 copy.87
  755.9 4.3 convert_bitcast_fusion.3
  771.4 157.7 %all-gather.17.cloned.1.call-done = bf16[2304,2,1152]{2,0,1:T(8,128)(2,1)} async-done(((bf16[576,2,1152]{2,0,1:T(8,128)(2,1)}), bf16[2304,2,1152]{2,0,1:T(8,128)(2,1)}) %all-gather.17.cloned.1.call-update) | async-done | bytes 10616848 | tf_op jit(solution)/shard_map/all_gather | solution.py:247
  929.1 5.2 convert_bitcast_fusion
  934.3 25.1 %copy.68 = f32[576,2,4,1152]{3,2,1,0:T(4,128)} copy(f32[576,2,4,1152]{3,0,2,1:T(8,128)S(1)} %convert_bitcast_fusion) | data formatting | bytes 42467328 | tf_op jit(solution)/shard_map/reshape | solution.py:324
  959.4 26.6 %reshape.272 = f32[576,2,4608]{2,1,0:T(2,128)} reshape(f32[576,2,4,1152]{3,2,1,0:T(4,128)} %copy.68) | data formatting | bytes 42467328 | tf_op jit(solution)/shard_map/reshape | solution.py:324
  (306 shorter events, 171.3 us)
Async XLA Ops:
  7.2 67.0 %all-gather.9.cloned.1.call-start = ((), (), s32[]{:S(2)}) async-start(), calls=%async_computation.3 | async-start | bytes 5898240 | tf_op jit(solution)/shard_map/all_gather | solution.py:170
  12.4 234.9 %all-gather.11.cloned.1.call-start = ((), (), s32[]{:S(2)}) async-start(), calls=%async_computation.4 | async-start | bytes 19906560 | tf_op jit(solution)/shard_map/all_gather | solution.py:176
  25.4 361.8 %reduce-scatter.6.cloned.1.call-start = ((), (), s32[]{:S(2)}) async-start(), calls=%async_computation.5 | async-start | bytes 6635520 | tf_op jit(solution)/shard_map/reduce_scatter | solution.py:242
  37.4 17.5 %collective-permute-start.7 = (bf16[64,2304]{1,0:T(8,128)(2,1)S(1)}, bf16[64,2304]{1,0:T(8,128)(2,1)S(1)}, u32[]{:S(2)}, u32[]{:S(2)}) collective-permute-start(bf16[64,2304]{1,0:T(8,128)(2,1)S(1)} %get-tuple-element.80), channel_id=1, source_target_pairs={{0,4},{2,6},{4,0},{6,2},{1,5},{3,7},{5,1},{7,3},{8,12},{10,14},{12... | collective-permute-start | bytes 884744 | tf_op jit(solution)/shard_map/ppermute | solution.py:48
  41.5 16.4 %collective-permute-start.6 = (bf16[64,2304]{1,0:T(8,128)(2,1)S(1)}, bf16[64,2304]{1,0:T(8,128)(2,1)S(1)}, u32[]{:S(2)}, u32[]{:S(2)}) collective-permute-start(bf16[64,2304]{1,0:T(8,128)(2,1)S(1)} %get-tuple-element.80), channel_id=1, source_target_pairs={{0,2},{2,0},{4,6},{6,4},{1,3},{3,1},{5,7},{7,5},{8,10},{10,8},{12,... | collective-permute-start | bytes 884744 | tf_op jit(solution)/shard_map/ppermute | solution.py:48
  54.9 8.1 collective-permute-start.8
  63.1 8.7 collective-permute-start.9
  66.3 14.2 %collective-permute-start = (s32[2,1,64]{2,0,1:T(2,128)S(1)}, s32[2,1,64]{2,0,1:T(2,128)S(1)}, u32[]{:S(2)}, u32[]{:S(2)}) collective-permute-start(s32[2,1,64]{2,0,1:T(2,128)S(1)} %broadcast_add_fusion), channel_id=1, source_target_pairs={{0,2},{2,0},{4,6},{6,4},{1,3},{3,1},{5,7},{7,5},{8,10},{10,8},{12,... | collective-permute-start | bytes 1544 | tf_op jit(solution)/shard_map/ppermute | solution.py:48
  68.1 12.5 %collective-permute-start.2 = (s32[2,1,64]{2,0,1:T(2,128)S(1)}, s32[2,1,64]{2,0,1:T(2,128)S(1)}, u32[]{:S(2)}, u32[]{:S(2)}) collective-permute-start(s32[2,1,64]{2,0,1:T(2,128)S(1)} %collective-permute-done.1), channel_id=1, source_target_pairs={{0,2},{2,0},{4,6},{6,4},{1,3},{3,1},{5,7},{7,5},{8,10},{10,8},{12,... | collective-permute-start | bytes 1544 | tf_op jit(solution)/shard_map/ppermute | solution.py:48
  78.9 23.0 %collective-permute-start.11 = (bf16[2,256,512]{2,1,0:T(8,128)(2,1)S(1)}, bf16[2,256,512]{2,1,0:T(8,128)(2,1)S(1)}, u32[]{:S(2)}, u32[]{:S(2)}) collective-permute-start(bf16[2,256,512]{2,1,0:T(8,128)(2,1)S(1)} %bitcast.132), channel_id=1, source_target_pairs={{0,16},{8,24},{16,0},{24,8},{1,17},{9,25},{17,1},{25,9},{2,18},{10... | collective-permute-start | bytes 1572872 | tf_op jit(solution)/shard_map/ppermute | solution.py:48
  80.6 16.3 %collective-permute-start.4 = (s32[2,1,256]{2,0,1:T(2,128)S(1)}, s32[2,1,256]{2,0,1:T(2,128)S(1)}, u32[]{:S(2)}, u32[]{:S(2)}) collective-permute-start(s32[2,1,256]{2,0,1:T(2,128)S(1)} %reshape.244), channel_id=1, source_target_pairs={{0,16},{8,24},{16,0},{24,8},{1,17},{9,25},{17,1},{25,9},{2,18},{10... | collective-permute-start | bytes 6152 | tf_op jit(solution)/shard_map/ppermute | solution.py:48
  81.1 17.1 %collective-permute-start.3 = (s32[2,1,256]{2,0,1:T(2,128)S(1)}, s32[2,1,256]{2,0,1:T(2,128)S(1)}, u32[]{:S(2)}, u32[]{:S(2)}) collective-permute-start(s32[2,1,256]{2,0,1:T(2,128)S(1)} %reshape.244), channel_id=1, source_target_pairs={{0,8},{8,0},{16,24},{24,16},{1,9},{9,1},{17,25},{25,17},{2,10},{10... | collective-permute-start | bytes 6152 | tf_op jit(solution)/shard_map/ppermute | solution.py:48
  100.6 26.1 %collective-permute-start.10 = (bf16[2,256,512]{2,1,0:T(8,128)(2,1)S(1)}, bf16[2,256,512]{2,1,0:T(8,128)(2,1)S(1)}, u32[]{:S(2)}, u32[]{:S(2)}) collective-permute-start(bf16[2,256,512]{2,1,0:T(8,128)(2,1)S(1)} %bitcast.133), channel_id=1, source_target_pairs={{0,8},{8,0},{16,24},{24,16},{1,9},{9,1},{17,25},{25,17},{2,10},{10... | collective-permute-start | bytes 1572872 | tf_op jit(solution)/shard_map/ppermute | solution.py:48
  102.0 44.9 %collective-permute-start.12 = (bf16[2,256,512]{2,1,0:T(8,128)(2,1)S(1)}, bf16[2,256,512]{2,1,0:T(8,128)(2,1)S(1)}, u32[]{:S(2)}, u32[]{:S(2)}) collective-permute-start(bf16[2,256,512]{2,1,0:T(8,128)(2,1)S(1)} %collective-permute-done.11), channel_id=1, source_target_pairs={{0,8},{8,0},{16,24},{24,16},{1,9},{9,1},{17,25},{25,17},{2,10},{10... | collective-permute-start | bytes 1572872 | tf_op jit(solution)/shard_map/ppermute | solution.py:48
  155.1 9.9 collective-permute-start.15
  155.2 20.8 %collective-permute-start.14 = (bf16[64,2304]{1,0:T(8,128)(2,1)S(1)}, bf16[64,2304]{1,0:T(8,128)(2,1)S(1)}, u32[]{:S(2)}, u32[]{:S(2)}) collective-permute-start(bf16[64,2304]{1,0:T(8,128)(2,1)S(1)} %get-tuple-element.98), channel_id=1, source_target_pairs={{0,2},{2,0},{4,6},{6,4},{1,3},{3,1},{5,7},{7,5},{8,10},{10,8},{12,... | collective-permute-start | bytes 884744 | tf_op jit(solution)/shard_map/ppermute | solution.py:48
  165.1 14.9 %collective-permute-start.16 = (bf16[64,2304]{1,0:T(8,128)(2,1)S(1)}, bf16[64,2304]{1,0:T(8,128)(2,1)S(1)}, u32[]{:S(2)}, u32[]{:S(2)}) collective-permute-start(bf16[64,2304]{1,0:T(8,128)(2,1)S(1)} %fusion.66), channel_id=1, source_target_pairs={{0,4},{2,6},{4,0},{6,2},{1,5},{3,7},{5,1},{7,3},{8,12},{10,14},{12... | collective-permute-start | bytes 884744 | tf_op jit(solution)/shard_map/ppermute | solution.py:48
  181.4 11.6 %collective-permute-start.18 = (bf16[64,2304]{1,0:T(8,128)(2,1)S(1)}, bf16[64,2304]{1,0:T(8,128)(2,1)S(1)}, u32[]{:S(2)}, u32[]{:S(2)}) collective-permute-start(bf16[64,2304]{1,0:T(8,128)(2,1)S(1)} %get-tuple-element.72), channel_id=1, source_target_pairs={{0,4},{2,6},{4,0},{6,2},{1,5},{3,7},{5,1},{7,3},{8,12},{10,14},{12... | collective-permute-start | bytes 884744 | tf_op jit(solution)/shard_map/ppermute | solution.py:48
  181.4 11.7 %collective-permute-start.17 = (bf16[64,2304]{1,0:T(8,128)(2,1)S(1)}, bf16[64,2304]{1,0:T(8,128)(2,1)S(1)}, u32[]{:S(2)}, u32[]{:S(2)}) collective-permute-start(bf16[64,2304]{1,0:T(8,128)(2,1)S(1)} %get-tuple-element.72), channel_id=1, source_target_pairs={{0,2},{2,0},{4,6},{6,4},{1,3},{3,1},{5,7},{7,5},{8,10},{10,8},{12,... | collective-permute-start | bytes 884744 | tf_op jit(solution)/shard_map/ppermute | solution.py:48
  193.0 6.7 collective-permute-start.19
  267.5 9.9 collective-permute-start.23
  269.1 19.1 %collective-permute-start.22 = (bf16[64,2304]{1,0:T(8,128)(2,1)S(1)}, bf16[64,2304]{1,0:T(8,128)(2,1)S(1)}, u32[]{:S(2)}, u32[]{:S(2)}) collective-permute-start(bf16[64,2304]{1,0:T(8,128)(2,1)S(1)} %get-tuple-element.96), channel_id=1, source_target_pairs={{0,2},{2,0},{4,6},{6,4},{1,3},{3,1},{5,7},{7,5},{8,10},{10,8},{12,... | collective-permute-start | bytes 884744 | tf_op jit(solution)/shard_map/ppermute | solution.py:48
  277.5 14.8 %collective-permute-start.24 = (bf16[64,2304]{1,0:T(8,128)(2,1)S(1)}, bf16[64,2304]{1,0:T(8,128)(2,1)S(1)}, u32[]{:S(2)}, u32[]{:S(2)}) collective-permute-start(bf16[64,2304]{1,0:T(8,128)(2,1)S(1)} %fusion.64), channel_id=1, source_target_pairs={{0,4},{2,6},{4,0},{6,2},{1,5},{3,7},{5,1},{7,3},{8,12},{10,14},{12... | collective-permute-start | bytes 884744 | tf_op jit(solution)/shard_map/ppermute | solution.py:48
  294.2 12.4 %collective-permute-start.27 = (bf16[64,2304]{1,0:T(8,128)(2,1)S(1)}, bf16[64,2304]{1,0:T(8,128)(2,1)S(1)}, u32[]{:S(2)}, u32[]{:S(2)}) collective-permute-start(bf16[64,2304]{1,0:T(8,128)(2,1)S(1)} %get-tuple-element.66), channel_id=1, source_target_pairs={{0,4},{2,6},{4,0},{6,2},{1,5},{3,7},{5,1},{7,3},{8,12},{10,14},{12... | collective-permute-start | bytes 884744 | tf_op jit(solution)/shard_map/ppermute | solution.py:48
  294.3 13.0 %collective-permute-start.26 = (bf16[64,2304]{1,0:T(8,128)(2,1)S(1)}, bf16[64,2304]{1,0:T(8,128)(2,1)S(1)}, u32[]{:S(2)}, u32[]{:S(2)}) collective-permute-start(bf16[64,2304]{1,0:T(8,128)(2,1)S(1)} %get-tuple-element.66), channel_id=1, source_target_pairs={{0,2},{2,0},{4,6},{6,4},{1,3},{3,1},{5,7},{7,5},{8,10},{10,8},{12,... | collective-permute-start | bytes 884744 | tf_op jit(solution)/shard_map/ppermute | solution.py:48
  306.6 7.6 collective-permute-start.28
  323.7 175.8 %reduce-scatter.8.cloned.1.call-start = ((), (), s32[]{:S(2)}) async-start(), calls=%async_computation.6 | async-start | bytes 13271040 | tf_op jit(solution)/shard_map/reduce_scatter | solution.py:242
  344.1 256.9 %all-gather.13.cloned.1.call-start = ((), (), s32[]{:S(2)}) async-start(), calls=%async_computation.7 | async-start | bytes 6635520 | tf_op jit(solution)/shard_map/all_gather | solution.py:247
  356.8 9.9 collective-permute-start.32
  358.6 19.2 %collective-permute-start.31 = (bf16[64,2304]{1,0:T(8,128)(2,1)S(1)}, bf16[64,2304]{1,0:T(8,128)(2,1)S(1)}, u32[]{:S(2)}, u32[]{:S(2)}) collective-permute-start(bf16[64,2304]{1,0:T(8,128)(2,1)S(1)} %get-tuple-element.94), channel_id=1, source_target_pairs={{0,2},{2,0},{4,6},{6,4},{1,3},{3,1},{5,7},{7,5},{8,10},{10,8},{12,... | collective-permute-start | bytes 884744 | tf_op jit(solution)/shard_map/ppermute | solution.py:48
  366.8 15.4 %collective-permute-start.33 = (bf16[64,2304]{1,0:T(8,128)(2,1)S(1)}, bf16[64,2304]{1,0:T(8,128)(2,1)S(1)}, u32[]{:S(2)}, u32[]{:S(2)}) collective-permute-start(bf16[64,2304]{1,0:T(8,128)(2,1)S(1)} %fusion.62), channel_id=1, source_target_pairs={{0,4},{2,6},{4,0},{6,2},{1,5},{3,7},{5,1},{7,3},{8,12},{10,14},{12... | collective-permute-start | bytes 884744 | tf_op jit(solution)/shard_map/ppermute | solution.py:48
  387.2 263.2 %reduce-scatter.10.cloned.1.call-start = ((), (), s32[]{:S(2)}) async-start(), calls=%async_computation.10 | async-start | bytes 4423680 | tf_op jit(solution)/shard_map/reduce_scatter | solution.py:303
  388.5 16.1 %collective-permute-start.35 = (bf16[64,2304]{1,0:T(8,128)(2,1)S(1)}, bf16[64,2304]{1,0:T(8,128)(2,1)S(1)}, u32[]{:S(2)}, u32[]{:S(2)}) collective-permute-start(bf16[64,2304]{1,0:T(8,128)(2,1)S(1)} %get-tuple-element.61), channel_id=1, source_target_pairs={{0,4},{2,6},{4,0},{6,2},{1,5},{3,7},{5,1},{7,3},{8,12},{10,14},{12... | collective-permute-start | bytes 884744 | tf_op jit(solution)/shard_map/ppermute | solution.py:48
  390.9 14.1 %collective-permute-start.34 = (bf16[64,2304]{1,0:T(8,128)(2,1)S(1)}, bf16[64,2304]{1,0:T(8,128)(2,1)S(1)}, u32[]{:S(2)}, u32[]{:S(2)}) collective-permute-start(bf16[64,2304]{1,0:T(8,128)(2,1)S(1)} %get-tuple-element.61), channel_id=1, source_target_pairs={{0,2},{2,0},{4,6},{6,4},{1,3},{3,1},{5,7},{7,5},{8,10},{10,8},{12,... | collective-permute-start | bytes 884744 | tf_op jit(solution)/shard_map/ppermute | solution.py:48
  404.6 7.9 collective-permute-start.36
  427.5 25.2 %collective-permute-start.38 = (bf16[2,1024,256]{2,1,0:T(8,128)(2,1)}, bf16[2,1024,256]{2,1,0:T(8,128)(2,1)S(1)}, u32[]{:S(2)}, u32[]{:S(2)}) collective-permute-start(bf16[2,1024,256]{2,1,0:T(8,128)(2,1)} %bitcast.141), channel_id=1, source_target_pairs={{0,2},{2,0},{4,6},{6,4},{1,3},{3,1},{5,7},{7,5},{8,10},{10,8},{12,... | collective-permute-start | bytes 3145736 | tf_op jit(solution)/shard_map/ppermute | solution.py:48
  453.2 9.3 collective-permute-start.40
  456.5 13.7 %collective-permute-start.39 = (bf16[2,256,256]{2,1,0:T(8,128)(2,1)S(1)}, bf16[2,256,256]{2,1,0:T(8,128)(2,1)S(1)}, u32[]{:S(2)}, u32[]{:S(2)}) collective-permute-start(bf16[2,256,256]{2,1,0:T(8,128)(2,1)S(1)} %get-tuple-element.102), channel_id=1, source_target_pairs={{0,8},{8,0},{16,24},{24,16},{1,9},{9,1},{17,25},{25,17},{2,10},{10... | collective-permute-start | bytes 786440 | tf_op jit(solution)/shard_map/ppermute | solution.py:48
  462.6 12.9 %collective-permute-start.41 = (bf16[2,256,256]{2,1,0:T(8,128)(2,1)S(1)}, bf16[2,256,256]{2,1,0:T(8,128)(2,1)S(1)}, u32[]{:S(2)}, u32[]{:S(2)}) collective-permute-start(bf16[2,256,256]{2,1,0:T(8,128)(2,1)S(1)} %fusion.69), channel_id=1, source_target_pairs={{0,16},{8,24},{16,0},{24,8},{1,17},{9,25},{17,1},{25,9},{2,18},{10... | collective-permute-start | bytes 786440 | tf_op jit(solution)/shard_map/ppermute | solution.py:48
  604.6 151.3 %all-gather.15.cloned.1.call-start = ((), (), s32[]{:S(2)}) async-start(), calls=%async_computation.8 | async-start | bytes 4423680 | tf_op jit(solution)/shard_map/all_gather | solution.py:247
  650.4 278.7 %all-gather.17.cloned.1.call-start = ((), (), s32[]{:S(2)}) async-start(), calls=%async_computation.9 | async-start | bytes 13271040 | tf_op jit(solution)/shard_map/all_gather | solution.py:247
  660.9 30.1 %collective-permute-start.44 = (bf16[64,2304]{1,0:T(8,128)(2,1)S(1)}, bf16[64,2304]{1,0:T(8,128)(2,1)S(1)}, u32[]{:S(2)}, u32[]{:S(2)}) collective-permute-start(bf16[64,2304]{1,0:T(8,128)(2,1)S(1)} %get-tuple-element.93), channel_id=1, source_target_pairs={{0,2},{2,0},{4,6},{6,4},{1,3},{3,1},{5,7},{7,5},{8,10},{10,8},{12,... | collective-permute-start | bytes 884744 | tf_op jit(solution)/shard_map/ppermute | solution.py:48
  662.5 45.6 %collective-permute-start.43 = (bf16[64,2304]{1,0:T(8,128)(2,1)S(1)}, bf16[64,2304]{1,0:T(8,128)(2,1)S(1)}, u32[]{:S(2)}, u32[]{:S(2)}) collective-permute-start(bf16[64,2304]{1,0:T(8,128)(2,1)S(1)} %get-tuple-element.92), channel_id=1, source_target_pairs={{0,2},{2,0},{4,6},{6,4},{1,3},{3,1},{5,7},{7,5},{8,10},{10,8},{12,... | collective-permute-start | bytes 884744 | tf_op jit(solution)/shard_map/ppermute | solution.py:48
  691.1 34.7 %collective-permute-start.45 = (bf16[64,2304]{1,0:T(8,128)(2,1)S(1)}, bf16[64,2304]{1,0:T(8,128)(2,1)S(1)}, u32[]{:S(2)}, u32[]{:S(2)}) collective-permute-start(bf16[64,2304]{1,0:T(8,128)(2,1)S(1)} %fusion.60), channel_id=1, source_target_pairs={{0,4},{2,6},{4,0},{6,2},{1,5},{3,7},{5,1},{7,3},{8,12},{10,14},{12... | collective-permute-start | bytes 884744 | tf_op jit(solution)/shard_map/ppermute | solution.py:48
  692.6 33.7 %collective-permute-start.25 = (bf16[64,2304]{1,0:T(8,128)(2,1)S(1)}, bf16[64,2304]{1,0:T(8,128)(2,1)S(1)}, u32[]{:S(2)}, u32[]{:S(2)}) collective-permute-start(bf16[64,2304]{1,0:T(8,128)(2,1)S(1)} %copy-done.14), channel_id=1, source_target_pairs={{0,1},{1,0},{2,3},{3,2},{4,5},{5,4},{6,7},{7,6},{8,9},{9,8},{10,11... | collective-permute-start | bytes 884744 | tf_op jit(solution)/shard_map/ppermute | solution.py:48
  732.9 8.4 collective-permute-start.49
  743.0 11.7 %collective-permute-start.46 = (f32[64,2304]{1,0:T(8,128)S(1)}, f32[64,2304]{1,0:T(8,128)S(1)}, u32[]{:S(2)}, u32[]{:S(2)}) collective-permute-start(f32[64,2304]{1,0:T(8,128)S(1)} %fusion.56), channel_id=1, source_target_pairs={{0,1},{1,0},{2,3},{3,2},{4,5},{5,4},{6,7},{7,6},{8,9},{9,8},{10,11... | collective-permute-start | bytes 1769480 | tf_op jit(solution)/shard_map/ppermute | solution.py:48
  745.4 8.7 collective-permute-start.51
  (50 other events, 833.0 us)
Sparse Core Ops, SparseCore 0:
  12.5 59.8 all-gather.8
  74.9 172.4 all-gather.10
  323.8 63.2 reduce-scatter.5
  390.7 108.7 reduce-scatter.7
  500.9 100.1 all-gather.12
  604.7 45.5 reduce-scatter.9
  651.9 89.6 all-gather.14
  743.8 185.1 all-gather.16

commit v3 on v2

--- a/solution.py
+++ b/solution.py
@@ -1,6 +1,8 @@
 import jax
 import jax.numpy as jnp
 from jax import lax
+from jax.experimental import pallas as pl
+from jax.experimental.pallas import tpu as pltpu
 from jax.sharding import PartitionSpec as P
 
 HEAD_DIM = 256
@@ -70,6 +72,24 @@
             held[j ^ offset] = held[j ^ offset].astype(F32) + got.astype(F32)
         offset *= 2
     return held[0]
+
+
+def gather_weights(part, own_at):
+    count = lax.axis_size("fsdp")
+    hops = [1 << i for i in range(count.bit_length() - 1)]
+    rows, width = part.shape
+    half = width // 2
+    whole = []
+    for columns, order in ((part[:, :half], hops), (part[:, half:], hops[::-1])):
+        held = {0: columns}
+        for offset in order:
+            for j in tuple(held):
+                held[j ^ offset] = swap(held[j], "fsdp", offset)
+        out = jnp.zeros((count * rows, columns.shape[1]), part.dtype)
+        for j in range(count):
+            out = lax.dynamic_update_slice_in_dim(out, held[j], (own_at ^ j) * rows, 0)
+        whole.append(out)
+    return whole
 
 
 def gather_rows(rows):
@@ -114,6 +134,35 @@
         values = picked.reshape(values.shape)
         offset *= 2
     return values
+
+
+def spread_columns(blocks, start, width, parts=1):
+    count, rows, _ = blocks.shape
+    each = width // parts
+    if each % 128 or start % width or rows % 96:
+        picked = blocks[:, :, start : start + width].reshape(count, rows, parts, each)
+        whole = jnp.moveaxis(picked, 0, 2).astype(F32).reshape(rows, parts, count * each)
+        return whole.reshape(rows, count * each) if parts == 1 else whole
+    step = 96
+
+    def kernel(in_ref, out_ref):
+        if parts == 1:
+            out_ref[...] = in_ref[...].astype(F32)
+        else:
+            for i in range(parts):
+                out_ref[:, i, :] = in_ref[:, i * each : (i + 1) * each].astype(F32)
+
+    shape = (rows, count * each) if parts == 1 else (rows, parts, count * each)
+    block = (step, each) if parts == 1 else (step, parts, each)
+    place = (lambda r, c: (r, c)) if parts == 1 else (lambda r, c: (r, 0, c))
+    return pl.pallas_call(
+        kernel,
+        out_shape=jax.ShapeDtypeStruct(shape, F32),
+        grid=(rows // step, count),
+        in_specs=[pl.BlockSpec((None, step, width), lambda r, c: (c, r, start // width))],
+        out_specs=pl.BlockSpec(block, place),
+        compiler_params=pltpu.CompilerParams(vmem_limit_bytes=32 << 20),
+    )(blocks)
 
 
 def cols(values, start, width):
@@ -157,6 +206,31 @@
     ff_width = ffn_out.shape[1] // ctx_count
     ff_at = ctx_at * ff_width
 
+    half_stretch = half_dev * fsdp_count
+    length = 2 * ctx_count * half_stretch
+    slot = jnp.arange(ctx_count) == ctx_at
+    paired = jnp.sum(jnp.where(slot, stretch_order, 0))
+    block = jnp.stack([paired, 2 * ctx_count - 1 - paired])
+    position = block[:, None] * half_stretch + fsdp_at * half_dev + jnp.arange(half_dev)
+    marks = segments.reshape(seq_count, 2, half_dev) * length + position[None]
+    slots = -(-ctx_count // 8) * 8
+    own_slot = jnp.arange(slots)[:, None] == ctx_at
+    placed = jnp.where(own_slot, marks.reshape(1, -1), 0).astype(F32)
+    mark_count = placed.shape[1]
+    placed = jnp.tile(placed, (ctx_count, pl.cdiv(512, mark_count)))
+    marks = lax.psum_scatter(placed, "ctx", scatter_dimension=0, tiled=True)
+    marks = marks[:ctx_count, :mark_count].astype(jnp.int32)
+    marks = marks.reshape(ctx_count, seq_count, 2 * half_dev).transpose(1, 0, 2)
+    marks = xor_order(marks, ctx_at, 1).reshape(seq_count, 1, -1)
+    marks = jnp.concatenate(gather_xor(marks, "fsdp"), axis=1)
+    marks = jnp.where(tp_at == 0, marks, jnp.flip(marks, 0))
+    query_mark = marks[:, 0]
+    key_mark = marks.reshape(seq_count, -1)
+    query_first = query_mark - lax.rem(query_mark, length)
+    allowed = (key_mark[:, None, :] <= query_mark[:, :, None]) & (
+        key_mark[:, None, :] >= query_first[:, :, None]
+    )
+
     kv_part = cols(keyval_proj, kv_at * HEAD_DIM, HEAD_DIM)
     att_part = jnp.concatenate(
         [
@@ -167,8 +241,8 @@
         ],
         axis=1,
     )
-    w_att = lax.all_gather(att_part, "fsdp", axis=0, tiled=True)
-    w_qkv, w_attn = w_att[:, : 3 * HEAD_DIM], w_att[:, 3 * HEAD_DIM :]
+    w_first, w_second = gather_weights(att_part, fsdp_at)
+    w_attn = w_second[:, HEAD_DIM:]
     in_part = cols(ffn_in, ff_at, ff_width)
     ffn_part = jnp.concatenate(
         [in_part[:, 0], in_part[:, 1], cols(ffn_out, ff_at, ff_width)], axis=1
@@ -185,26 +259,9 @@
         cotangent.reshape(row_count, width), row_at, own_count, 0
     ).astype(F32)
 
-    half_stretch = half_dev * fsdp_count
-    length = 2 * ctx_count * half_stretch
-    slot = jnp.arange(ctx_count) == ctx_at
-    paired = jnp.sum(jnp.where(slot, stretch_order, 0))
-    block = jnp.stack([paired, 2 * ctx_count - 1 - paired])
-    position = block[:, None] * half_stretch + fsdp_at * half_dev + jnp.arange(half_dev)
-    marks = segments.reshape(seq_count, 2, half_dev) * length + position[None]
-    marks = marks.reshape(seq_count, 1, 2 * half_dev)
-    marks = jnp.concatenate(gather_xor(marks, "ctx"), axis=1).reshape(seq_count, 1, -1)
-    marks = jnp.concatenate(gather_xor(marks, "fsdp"), axis=1)
-    marks = jnp.where(tp_at == 0, marks, jnp.flip(marks, 0))
-    query_mark = marks[:, 0]
-    key_mark = marks.reshape(seq_count, -1)
-    query_first = query_mark - lax.rem(query_mark, length)
-    allowed = (key_mark[:, None, :] <= query_mark[:, :, None]) & (
-        key_mark[:, None, :] >= query_first[:, :, None]
-    )
-
     xnorm_own = (tok_in * rms_factor(tok_in) * gain_pre).astype(BF16)
     xnorm = gather_rows(xnorm_own)
+    w_qkv = jnp.concatenate([w_first, w_second[:, :HEAD_DIM]], axis=1)
     qkv = dot_nn(xnorm, w_qkv).astype(BF16)
     query = qkv[:, :HEAD_DIM].reshape(seq_count, -1, HEAD_DIM)
     kv_own_rows = qkv[:, HEAD_DIM:].reshape(seq_count, -1, 2 * HEAD_DIM)
@@ -285,9 +342,7 @@
     grad_q = grad_q.reshape(group_rows, HEAD_DIM)
     grad_q_own = grad_q if repeat == 1 else cols(grad_q, q_own, q_width)
     grad_qkv = jnp.concatenate([grad_q_own, grad_kv], axis=1)
-    grad_qkv = after(grad_qkv, part_in)
-    own_width = part_in.shape[0]
-    part_in = jnp.stack([part_in[:, :ff_width], part_in[:, ff_width:]], axis=1)
+    grad_qkv = after(grad_qkv, part_in, all_out)
     all_in = spread(part_in)
     w_q_own = w_qkv[:, :HEAD_DIM] if repeat == 1 else cols(w_qkv, q_own, q_width)
     w_qkv_own = jnp.concatenate([w_q_own, cols(w_qkv, HEAD_DIM + kv_own, kv_width)], axis=1)
@@ -299,9 +354,8 @@
         [dot_tn(xnorm, grad_qkv).astype(BF16), dot_tn(grad_branchb, attended_own).astype(BF16)],
         axis=1,
     )
-    att_term = after(att_term, all_out)
-    all_att = spread(lax.psum_scatter(att_term, "fsdp", scatter_dimension=0, tiled=True))
-    all_qkv, all_attn = all_att[:, :, : q_width + kv_width], all_att[:, :, q_width + kv_width :]
+    part_att = lax.psum_scatter(att_term, "fsdp", scatter_dimension=0, tiled=True)
+    all_att = spread(after(part_att, all_in))
 
     grad_gains = sum_all(
         jnp.stack([grad_pre_gain, grad_post_gain, grad_ffn_gain, grad_last_gain], axis=0)
@@ -309,20 +363,18 @@
     result = both_cores(result, tp_at)
     grad_tokens = both_cores(grad_tokens_own, tp_at)
 
-    def columns(spread_grad):
-        return jnp.moveaxis(spread_grad, 0, -2).astype(F32)
-
-    grad_query = columns(all_qkv[:, :, :q_width]).reshape(own_width, -1)
+    grad_ffn_in = spread_columns(all_in, 0, 2 * ff_width, 2)
+    grad_ffn_out = spread_columns(all_out, 0, ff_width)
+    grad_query = spread_columns(all_att, 0, q_width)
+    grad_attn = spread_columns(all_att, q_width + kv_width, q_width)
+    own_width = all_att.shape[1]
     grad_keyval = (
-        all_qkv[:, :, q_width:]
+        all_att[:, :, q_width : q_width + kv_width]
         .reshape(ctx_count // sharers, 2, sharers // 2, own_width, kv_width)
         .transpose(3, 1, 0, 2, 4)
         .astype(F32)
         .reshape(own_width, 2, -1)
     )
-    grad_attn = columns(all_attn).reshape(own_width, -1)
-    grad_ffn_in = columns(all_in).reshape(own_width, 2, -1)
-    grad_ffn_out = columns(all_out).reshape(own_width, -1)
     return (
         result.reshape(tokens.shape),
         grad_tokens.reshape(tokens.shape),

time: 1000 us -> 904 us (0.904)
  waiting for transfers between devices: 690 us -> 635 us
  local copies, waits for them, and re-layouts: 114 us -> 65.4 us
  Pallas kernels: 0 us -> 39 us
  starting transfers between devices: 75.4 us -> 50.9 us
    all_gather x3, waiting for transfers between devices: 258 us -> 172 us  [spread(): return lax.all_gather(part, 'ctx', axis=0, tiled=False)]
    ppermute x52 -> x55, waiting for transfers between devices: 316 us -> 381 us  [swap(): lax.ppermute(values, axis_name, [(i, i ^ offset) for i in range(count)])]
    reshape x6 -> x3, local copies, waits for them, and re-layouts: 63.6 us -> 5.65 us  [the longest x2 5.56 us: on_device(): grad_keyval = all_att[:, :, q_width:q_width + kv_width].reshape(ctx_count...]
    reduce_scatter x1, waiting for transfers between devices: 45.7 us -> 0.01 us  [on_device(): marks = lax.psum_scatter(placed, 'ctx', scatter_dimension=0, tiled=True)]
    all_gather x1, waiting for transfers between devices: 43.6 us -> 0.01 us  [on_device(): w_ffn = lax.all_gather(ffn_part, 'fsdp', axis=0, tiled=True)]
    pallas_call x0 -> x4, Pallas kernels: none -> 39 us  [spread_columns(): pl.pallas_call(kernel, out_shape=jax.ShapeDtypeStruct(shape, F32), grid=(...]
    reduce_scatter x2, waiting for transfers between devices: 26.8 us -> 59.6 us  [weight_grad(): lax.psum_scatter(dot_tn(left, right).astype(BF16), 'fsdp', scatter_dimens...]
    unnamed x8 -> x9, waiting for transfers between devices: 0.13 us -> 22.3 us
  transfers between devices with their start and end apart: 60 -> 63, of which waited for: 45 -> 49; matrix products, arithmetic and copies ran while one was open for 11% -> 11% of each run, Pallas kernels for 0% -> 3%
where the time goes in v3:
time: 904 us; the launch traced here: 897 us
  waiting for transfers between devices  635 us (70%)
  local copies, waits for them, and re-layouts  65.4 us (7%)
  matrix products  63.1 us (7%)
  starting transfers between devices  50.9 us (6%)
  Pallas kernels  39 us (4%)
  other arithmetic  26.4 us (3%)
  between operations  17.6 us (2%)
    ppermute x55, waiting for transfers between devices, swap(): lax.ppermute(values, axis_name, [(i, i ^ offset) for i in range(count)])  381 us
    all_gather x3, waiting for transfers between devices, spread(): return lax.all_gather(part, 'ctx', axis=0, tiled=False)  172 us
    reduce_scatter x2, waiting for transfers between devices, weight_grad(): lax.psum_scatter(dot_tn(left, right).astype(BF16), 'fsdp', scatter_dimens...  59.6 us
    ppermute x55, starting transfers between devices, swap(): lax.ppermute(values, axis_name, [(i, i ^ offset) for i in range(count)])  49.9 us
    pallas_call x4, Pallas kernels, spread_columns(): pl.pallas_call(kernel, out_shape=jax.ShapeDtypeStruct(shape, F32), grid=(...  39 us
    unnamed x144, local copies, waits for them, and re-layouts  26.3 us
    unnamed x9, waiting for transfers between devices  22.3 us
    dot_general x4, matrix products, dot_nn(): return jnp.dot(left, right, preferred_element_type=F32)  22.3 us
  transfers between devices with their start and end apart: 63, of which 49 were waited for; matrix products, arithmetic and copies ran while one was open for 11% of the time, Pallas kernels for 3%

profile of v3, /device:TPU:0, one launch (start us, length us, event | category | flops | bytes accessed | tf_op | source)
XLA Modules:
  0.0 897.0 jit_solution(2023518319178849275)
XLA Ops:
  13.9 8.9 constant_dynamic-slice_fusion
  48.0 5.9 collective-permute-done.5
  54.8 13.0 %collective-permute-done.11 = bf16[576,512]{1,0:T(8,128)(2,1)} collective-permute-done((bf16[576,512]{1,0:T(8,128)(2,1)}, bf16[576,512]{1,0:T(8,128)(2,1)}, u32[]{:S(2)}, u32[]{:S(2)}) %collective-permute-start.11) | collective-permute-done | bytes 589856 | tf_op jit(solution)/shard_map/ppermute | solution.py:50
  68.4 23.1 %collective-permute-done.7 = bf16[576,512]{1,0:T(8,128)(2,1)} collective-permute-done((bf16[576,512]{1,0:T(8,128)(2,1)}, bf16[576,512]{1,0:T(8,128)(2,1)}, u32[]{:S(2)}, u32[]{:S(2)}) %collective-permute-start.7) | collective-permute-done | bytes 589856 | tf_op jit(solution)/shard_map/ppermute | solution.py:50
  96.4 18.3 %collective-permute-done.12 = bf16[576,512]{1,0:T(8,128)(2,1)S(1)} collective-permute-done((bf16[576,512]{1,0:T(8,128)(2,1)}, bf16[576,512]{1,0:T(8,128)(2,1)S(1)}, u32[]{:S(2)}, u32[]{:S(2)}) %collective-permute-start.12) | collective-permute-done | bytes 589856 | tf_op jit(solution)/shard_map/ppermute | solution.py:50
  125.3 13.7 %collective-permute-done.1 = s32[2,1,256]{2,0,1:T(2,128)S(1)} collective-permute-done((s32[2,1,256]{2,0,1:T(2,128)S(1)}, s32[2,1,256]{2,0,1:T(2,128)S(1)}, u32[]{:S(2)}, u32[]{:S(2)}) %collective-permute-start.1) | collective-permute-done | bytes 2080 | tf_op jit(solution)/shard_map/ppermute | solution.py:50
  139.0 3.6 collective-permute-done.2
  146.3 22.9 %collective-permute-done.13 = bf16[2,256,512]{2,1,0:T(8,128)(2,1)S(1)} collective-permute-done((bf16[2,256,512]{2,1,0:T(8,128)(2,1)S(1)}, bf16[2,256,512]{2,1,0:T(8,128)(2,1)S(1)}, u32[]{:S(2)}, u32[]{:S(2)}) %collective-permute-start.13) | collective-permute-done | bytes 524320 | tf_op jit(solution)/shard_map/ppermute | solution.py:50
  169.3 18.5 %collective-permute-done.15 = bf16[2,256,512]{2,1,0:T(8,128)(2,1)S(1)} collective-permute-done((bf16[2,256,512]{2,1,0:T(8,128)(2,1)S(1)}, bf16[2,256,512]{2,1,0:T(8,128)(2,1)S(1)}, u32[]{:S(2)}, u32[]{:S(2)}) %collective-permute-start.15) | collective-permute-done | bytes 524320 | tf_op jit(solution)/shard_map/ppermute | solution.py:50
  198.1 7.8 collective-permute-done.18
  206.1 6.0 collective-permute-done.17
  212.1 11.9 %collective-permute-done.19 = bf16[64,2304]{1,0:T(8,128)(2,1)S(1)} collective-permute-done((bf16[64,2304]{1,0:T(8,128)(2,1)S(1)}, bf16[64,2304]{1,0:T(8,128)(2,1)S(1)}, u32[]{:S(2)}, u32[]{:S(2)}) %collective-permute-start.19) | collective-permute-done | bytes 294944 | tf_op jit(solution)/shard_map/ppermute | solution.py:50
  225.4 9.5 %collective-permute-done.21 = bf16[64,2304]{1,0:T(8,128)(2,1)S(1)} collective-permute-done((bf16[64,2304]{1,0:T(8,128)(2,1)S(1)}, bf16[64,2304]{1,0:T(8,128)(2,1)S(1)}, u32[]{:S(2)}, u32[]{:S(2)}) %collective-permute-start.21) | collective-permute-done | bytes 294944 | tf_op jit(solution)/shard_map/ppermute | solution.py:50
  234.9 6.3 collective-permute-done.20
  241.2 5.1 collective-permute-done.22
  250.5 8.8 fusion.2
  261.4 5.8 fusion.6
  272.7 7.8 collective-permute-done.26
  280.7 5.5 collective-permute-done.25
  286.1 12.1 %collective-permute-done.27 = bf16[64,2304]{1,0:T(8,128)(2,1)S(1)} collective-permute-done((bf16[64,2304]{1,0:T(8,128)(2,1)S(1)}, bf16[64,2304]{1,0:T(8,128)(2,1)S(1)}, u32[]{:S(2)}, u32[]{:S(2)}) %collective-permute-start.27) | collective-permute-done | bytes 294944 | tf_op jit(solution)/shard_map/ppermute | solution.py:50
  300.4 9.8 %collective-permute-done.30 = bf16[64,2304]{1,0:T(8,128)(2,1)S(1)} collective-permute-done((bf16[64,2304]{1,0:T(8,128)(2,1)S(1)}, bf16[64,2304]{1,0:T(8,128)(2,1)S(1)}, u32[]{:S(2)}, u32[]{:S(2)}) %collective-permute-start.30) | collective-permute-done | bytes 294944 | tf_op jit(solution)/shard_map/ppermute | solution.py:50
  310.3 6.3 collective-permute-done.29
  316.6 5.4 collective-permute-done.31
  326.5 5.0 convolution_convert_fusion.1
  331.7 59.5 %reduce-scatter.9.cloned.1.call-done = bf16[576,1152]{1,0:T(8,128)(2,1)} async-done(((bf16[2304,1152]{1,0:T(8,128)(2,1)}), bf16[576,1152]{1,0:T(8,128)(2,1)}) %reduce-scatter.9.cloned.1.call-update) | async-done | bytes 1327120 | tf_op jit(solution)/shard_map/reduce_scatter | solution.py:299
  391.3 8.9 fusion.16
  401.6 9.9 %convolution_convert_fusion = bf16[2304,2304]{1,0:T(8,128)(2,1)} fusion(bf16[512,2304]{1,0:T(8,128)(2,1)} %constant_dynamic-update-slice_fusion.9, bf16[512,1152]{1,0:T(8,128)(2,1)S(1)} %get-tuple-element.76, bf16[512,1152]{1,0:T(8,128)(2,1)S(1)} %get-tuple-element.75), kind=kOutput, calls=%fused_computation | convolution fusion | flops 5445844992 | bytes 15335424 | tf_op jit(solution)/shard_map/dot_general | solution.py:45
  411.6 9.1 %fusion = f32[512,2304]{1,0:T(8,128)S(1)} fusion(bf16[2304,3456]{1,0:T(8,128)(2,1)} %all-gather.8.cloned.1.call-done, bf16[512,1152]{1,0:T(8,128)(2,1)} %copy-done.60, bf16[512,1152]{1,0:T(8,128)(2,1)} %copy-done.59), kind=kOutput, calls=%fused_computation.2 | convolution fusion | flops 5440536576 | bytes 17694720 | tf_op jit(solution)/shard_map/dot_general | solution.py:41
  426.2 35.2 %collective-permute-done.35 = bf16[64,2304]{1,0:T(8,128)(2,1)S(1)} collective-permute-done((bf16[64,2304]{1,0:T(8,128)(2,1)S(1)}, bf16[64,2304]{1,0:T(8,128)(2,1)S(1)}, u32[]{:S(2)}, u32[]{:S(2)}) %collective-permute-start.35) | collective-permute-done | bytes 294944 | tf_op jit(solution)/shard_map/ppermute | solution.py:50
  461.6 19.3 %collective-permute-done.34 = bf16[64,2304]{1,0:T(8,128)(2,1)S(1)} collective-permute-done((bf16[64,2304]{1,0:T(8,128)(2,1)S(1)}, bf16[64,2304]{1,0:T(8,128)(2,1)S(1)}, u32[]{:S(2)}, u32[]{:S(2)}) %collective-permute-start.34) | collective-permute-done | bytes 294944 | tf_op jit(solution)/shard_map/ppermute | solution.py:50
  481.0 14.0 %collective-permute-done.36 = bf16[64,2304]{1,0:T(8,128)(2,1)S(1)} collective-permute-done((bf16[64,2304]{1,0:T(8,128)(2,1)S(1)}, bf16[64,2304]{1,0:T(8,128)(2,1)S(1)}, u32[]{:S(2)}, u32[]{:S(2)}) %collective-permute-start.36) | collective-permute-done | bytes 294944 | tf_op jit(solution)/shard_map/ppermute | solution.py:50
  497.8 6.2 collective-permute-start.37
  504.0 13.6 %collective-permute-done.38 = bf16[64,2304]{1,0:T(8,128)(2,1)S(1)} collective-permute-done((bf16[64,2304]{1,0:T(8,128)(2,1)S(1)}, bf16[64,2304]{1,0:T(8,128)(2,1)S(1)}, u32[]{:S(2)}, u32[]{:S(2)}) %collective-permute-start.38) | collective-permute-done | bytes 294944 | tf_op jit(solution)/shard_map/ppermute | solution.py:50
  519.8 6.1 collective-permute-done.39
  542.2 24.8 %collective-permute-done.41 = bf16[2,1024,256]{2,1,0:T(8,128)(2,1)S(1)} collective-permute-done((bf16[2,1024,256]{2,1,0:T(8,128)(2,1)}, bf16[2,1024,256]{2,1,0:T(8,128)(2,1)S(1)}, u32[]{:S(2)}, u32[]{:S(2)}) %collective-permute-start.41) | collective-permute-done | bytes 1048608 | tf_op jit(solution)/shard_map/ppermute | solution.py:50
  571.3 5.4 collective-permute-done.43
  585.8 3.6 copy.50
  600.2 10.5 %collective-permute-done.47 = bf16[64,2304]{1,0:T(8,128)(2,1)S(1)} collective-permute-done((bf16[64,2304]{1,0:T(8,128)(2,1)S(1)}, bf16[64,2304]{1,0:T(8,128)(2,1)S(1)}, u32[]{:S(2)}, u32[]{:S(2)}) %collective-permute-start.47) | collective-permute-done | bytes 294944 | tf_op jit(solution)/shard_map/ppermute | solution.py:50
  611.4 5.4 collective-permute-start.48
  616.8 21.5 %reduce-scatter.13.cloned.1.call-done = bf16[576,768]{1,0:T(8,128)(2,1)} async-done(((bf16[2304,768]{1,0:T(8,128)(2,1)}), bf16[576,768]{1,0:T(8,128)(2,1)}) %reduce-scatter.13.cloned.1.call-update) | async-done | bytes 884752
  640.6 152.2 %all-gather.12.cloned.1.call-done = bf16[2304,2304]{1,0:T(8,128)(2,1)} async-done(((bf16[576,2304]{1,0:T(8,128)(2,1)}), bf16[2304,2304]{1,0:T(8,128)(2,1)}) %all-gather.12.cloned.1.call-update) | async-done | bytes 10616848 | tf_op jit(solution)/shard_map/all_gather | solution.py:304
  806.7 4.7 collective-permute-done.52
  821.0 9.6 %shard_map.164 = f32[576,4608]{1,0:T(8,128)} custom-call(bf16[4,576,1152]{2,1,0:T(8,128)(2,1)S(1)} %bitcast.106), custom_call_target="tpu_custom_call" | custom-call | tf_op jit(solution)/shard_map/pallas_call | solution.py:158
  832.5 13.7 %shard_map.163 = f32[576,2,4608]{2,1,0:T(2,128)} custom-call(bf16[4,576,2304]{2,1,0:T(8,128)(2,1)S(1)} %bitcast.105), custom_call_target="tpu_custom_call" | custom-call | tf_op jit(solution)/shard_map/pallas_call | solution.py:158
  846.1 19.7 %all-gather.14.cloned.1.call-done = bf16[2304,768]{1,0:T(8,128)(2,1)} async-done(((bf16[576,768]{1,0:T(8,128)(2,1)}), bf16[2304,768]{1,0:T(8,128)(2,1)}) %all-gather.14.cloned.1.call-update) | async-done | bytes 3538960 | tf_op jit(solution)/shard_map/all_gather | solution.py:304
  867.8 7.8 shard_map.161
  875.8 7.9 shard_map.162
  885.7 3.7 reshape.256
  (374 shorter events, 166.0 us)
Async XLA Ops:
  8.0 34.0 %reduce-scatter.7.cloned.1.call-start = ((), (), s32[]{:S(2)}) async-start(), calls=%async_computation.4 | async-start | bytes 81920 | tf_op jit(solution)/shard_map/reduce_scatter | solution.py:221
  12.4 238.0 %all-gather.8.cloned.1.call-start = ((), (), s32[]{:S(2)}) async-start(), calls=%async_computation.5 | async-start | bytes 19906560 | tf_op jit(solution)/shard_map/all_gather | solution.py:250
  25.4 365.8 %reduce-scatter.9.cloned.1.call-start = ((), (), s32[]{:S(2)}) async-start(), calls=%async_computation.6 | async-start | bytes 6635520 | tf_op jit(solution)/shard_map/reduce_scatter | solution.py:299
  28.1 16.3 %collective-permute-start.3 = (bf16[64,2304]{1,0:T(8,128)(2,1)S(1)}, bf16[64,2304]{1,0:T(8,128)(2,1)S(1)}, u32[]{:S(2)}, u32[]{:S(2)}) collective-permute-start(bf16[64,2304]{1,0:T(8,128)(2,1)S(1)} %get-tuple-element.72), channel_id=1, source_target_pairs={{0,2},{2,0},{4,6},{6,4},{1,3},{3,1},{5,7},{7,5},{8,10},{10,8},{12,... | collective-permute-start | bytes 884744 | tf_op jit(solution)/shard_map/ppermute | solution.py:50
  31.1 15.7 %collective-permute-start.4 = (bf16[64,2304]{1,0:T(8,128)(2,1)S(1)}, bf16[64,2304]{1,0:T(8,128)(2,1)S(1)}, u32[]{:S(2)}, u32[]{:S(2)}) collective-permute-start(bf16[64,2304]{1,0:T(8,128)(2,1)S(1)} %get-tuple-element.72), channel_id=1, source_target_pairs={{0,4},{2,6},{4,0},{6,2},{1,5},{3,7},{5,1},{7,3},{8,12},{10,14},{12... | collective-permute-start | bytes 884744 | tf_op jit(solution)/shard_map/ppermute | solution.py:50
  37.6 56.5 %collective-permute-start.10 = (bf16[576,512]{1,0:T(8,128)(2,1)}, bf16[576,512]{1,0:T(8,128)(2,1)}, u32[]{:S(2)}, u32[]{:S(2)}) collective-permute-start(bf16[576,512]{1,0:T(8,128)(2,1)} %get-tuple-element.98), channel_id=1, source_target_pairs={{0,8},{8,0},{16,24},{24,16},{1,9},{9,1},{17,25},{25,17},{2,10},{10... | collective-permute-start | bytes 1769480 | tf_op jit(solution)/shard_map/ppermute | solution.py:50
  38.9 28.9 %collective-permute-start.11 = (bf16[576,512]{1,0:T(8,128)(2,1)}, bf16[576,512]{1,0:T(8,128)(2,1)}, u32[]{:S(2)}, u32[]{:S(2)}) collective-permute-start(bf16[576,512]{1,0:T(8,128)(2,1)} %get-tuple-element.98), channel_id=1, source_target_pairs={{0,16},{8,24},{16,0},{24,8},{1,17},{9,25},{17,1},{25,9},{2,18},{10... | collective-permute-start | bytes 1769480 | tf_op jit(solution)/shard_map/ppermute | solution.py:50
  41.5 49.9 %collective-permute-start.7 = (bf16[576,512]{1,0:T(8,128)(2,1)}, bf16[576,512]{1,0:T(8,128)(2,1)}, u32[]{:S(2)}, u32[]{:S(2)}) collective-permute-start(bf16[576,512]{1,0:T(8,128)(2,1)} %get-tuple-element.96), channel_id=1, source_target_pairs={{0,8},{8,0},{16,24},{24,16},{1,9},{9,1},{17,25},{25,17},{2,10},{10... | collective-permute-start | bytes 1769480 | tf_op jit(solution)/shard_map/ppermute | solution.py:50
  44.4 51.9 %collective-permute-start.8 = (bf16[576,512]{1,0:T(8,128)(2,1)}, bf16[576,512]{1,0:T(8,128)(2,1)S(1)}, u32[]{:S(2)}, u32[]{:S(2)}) collective-permute-start(bf16[576,512]{1,0:T(8,128)(2,1)} %get-tuple-element.96), channel_id=1, source_target_pairs={{0,16},{8,24},{16,0},{24,8},{1,17},{9,25},{17,1},{25,9},{2,18},{10... | collective-permute-start | bytes 1769480 | tf_op jit(solution)/shard_map/ppermute | solution.py:50
  54.0 64.4 %collective-permute-start.6 = (bf16[256,2304]{1,0:T(8,128)(2,1)S(1)}, bf16[256,2304]{1,0:T(8,128)(2,1)S(1)}, u32[]{:S(2)}, u32[]{:S(2)}) collective-permute-start(bf16[256,2304]{1,0:T(8,128)(2,1)S(1)} %pad_maximum_fusion.10), channel_id=1, source_target_pairs={{0,1},{1,0},{2,3},{3,2},{4,5},{5,4},{6,7},{7,6},{8,9},{9,8},{10,11... | collective-permute-start | bytes 3538952 | tf_op jit(solution)/shard_map/ppermute | solution.py:50
  67.8 46.9 %collective-permute-start.12 = (bf16[576,512]{1,0:T(8,128)(2,1)}, bf16[576,512]{1,0:T(8,128)(2,1)S(1)}, u32[]{:S(2)}, u32[]{:S(2)}) collective-permute-start(bf16[576,512]{1,0:T(8,128)(2,1)} %collective-permute-done.11), channel_id=1, source_target_pairs={{0,8},{8,0},{16,24},{24,16},{1,9},{9,1},{17,25},{25,17},{2,10},{10... | collective-permute-start | bytes 1769480 | tf_op jit(solution)/shard_map/ppermute | solution.py:50
  91.4 26.9 %collective-permute-start.9 = (bf16[576,512]{1,0:T(8,128)(2,1)}, bf16[576,512]{1,0:T(8,128)(2,1)S(1)}, u32[]{:S(2)}, u32[]{:S(2)}) collective-permute-start(bf16[576,512]{1,0:T(8,128)(2,1)} %collective-permute-done.7), channel_id=1, source_target_pairs={{0,16},{8,24},{16,0},{24,8},{1,17},{9,25},{17,1},{25,9},{2,18},{10... | collective-permute-start | bytes 1769480 | tf_op jit(solution)/shard_map/ppermute | solution.py:50
  121.5 21.8 %collective-permute-start.14 = (bf16[2,256,512]{2,1,0:T(8,128)(2,1)S(1)}, bf16[2,256,512]{2,1,0:T(8,128)(2,1)S(1)}, u32[]{:S(2)}, u32[]{:S(2)}) collective-permute-start(bf16[2,256,512]{2,1,0:T(8,128)(2,1)S(1)} %bitcast.117), channel_id=1, source_target_pairs={{0,16},{8,24},{16,0},{24,8},{1,17},{9,25},{17,1},{25,9},{2,18},{10... | collective-permute-start | bytes 1572872 | tf_op jit(solution)/shard_map/ppermute | solution.py:50
  123.5 15.5 %collective-permute-start = (s32[2,1,256]{2,0,1:T(2,128)S(1)}, s32[2,1,256]{2,0,1:T(2,128)S(1)}, u32[]{:S(2)}, u32[]{:S(2)}) collective-permute-start(s32[2,1,256]{2,0,1:T(2,128)S(1)} %reshape_reshape.8), channel_id=1, source_target_pairs={{0,8},{8,0},{16,24},{24,16},{1,9},{9,1},{17,25},{25,17},{2,10},{10... | collective-permute-start | bytes 6152 | tf_op jit(solution)/shard_map/ppermute | solution.py:50
  125.1 13.9 %collective-permute-start.1 = (s32[2,1,256]{2,0,1:T(2,128)S(1)}, s32[2,1,256]{2,0,1:T(2,128)S(1)}, u32[]{:S(2)}, u32[]{:S(2)}) collective-permute-start(s32[2,1,256]{2,0,1:T(2,128)S(1)} %reshape_reshape.8), channel_id=1, source_target_pairs={{0,16},{8,24},{16,0},{24,8},{1,17},{9,25},{17,1},{25,9},{2,18},{10... | collective-permute-start | bytes 6152 | tf_op jit(solution)/shard_map/ppermute | solution.py:50
  143.2 26.1 %collective-permute-start.13 = (bf16[2,256,512]{2,1,0:T(8,128)(2,1)S(1)}, bf16[2,256,512]{2,1,0:T(8,128)(2,1)S(1)}, u32[]{:S(2)}, u32[]{:S(2)}) collective-permute-start(bf16[2,256,512]{2,1,0:T(8,128)(2,1)S(1)} %bitcast.118), channel_id=1, source_target_pairs={{0,8},{8,0},{16,24},{24,16},{1,9},{9,1},{17,25},{25,17},{2,10},{10... | collective-permute-start | bytes 1572872 | tf_op jit(solution)/shard_map/ppermute | solution.py:50
  143.3 44.5 %collective-permute-start.15 = (bf16[2,256,512]{2,1,0:T(8,128)(2,1)S(1)}, bf16[2,256,512]{2,1,0:T(8,128)(2,1)S(1)}, u32[]{:S(2)}, u32[]{:S(2)}) collective-permute-start(bf16[2,256,512]{2,1,0:T(8,128)(2,1)S(1)} %collective-permute-done.14), channel_id=1, source_target_pairs={{0,8},{8,0},{16,24},{24,16},{1,9},{9,1},{17,25},{25,17},{2,10},{10... | collective-permute-start | bytes 1572872 | tf_op jit(solution)/shard_map/ppermute | solution.py:50
  196.0 9.9 %collective-permute-start.18 = (bf16[64,2304]{1,0:T(8,128)(2,1)S(1)}, bf16[64,2304]{1,0:T(8,128)(2,1)S(1)}, u32[]{:S(2)}, u32[]{:S(2)}) collective-permute-start(bf16[64,2304]{1,0:T(8,128)(2,1)S(1)} %get-tuple-element.88), channel_id=1, source_target_pairs={{0,2},{2,0},{4,6},{6,4},{1,3},{3,1},{5,7},{7,5},{8,10},{10,8},{12,... | collective-permute-start | bytes 884744 | tf_op jit(solution)/shard_map/ppermute | solution.py:50
  196.1 16.0 %collective-permute-start.17 = (bf16[64,2304]{1,0:T(8,128)(2,1)S(1)}, bf16[64,2304]{1,0:T(8,128)(2,1)S(1)}, u32[]{:S(2)}, u32[]{:S(2)}) collective-permute-start(bf16[64,2304]{1,0:T(8,128)(2,1)S(1)} %get-tuple-element.87), channel_id=1, source_target_pairs={{0,2},{2,0},{4,6},{6,4},{1,3},{3,1},{5,7},{7,5},{8,10},{10,8},{12,... | collective-permute-start | bytes 884744 | tf_op jit(solution)/shard_map/ppermute | solution.py:50
  206.0 18.0 %collective-permute-start.19 = (bf16[64,2304]{1,0:T(8,128)(2,1)S(1)}, bf16[64,2304]{1,0:T(8,128)(2,1)S(1)}, u32[]{:S(2)}, u32[]{:S(2)}) collective-permute-start(bf16[64,2304]{1,0:T(8,128)(2,1)S(1)} %fusion.69), channel_id=1, source_target_pairs={{0,4},{2,6},{4,0},{6,2},{1,5},{3,7},{5,1},{7,3},{8,12},{10,14},{12... | collective-permute-start | bytes 884744 | tf_op jit(solution)/shard_map/ppermute | solution.py:50
  225.4 9.5 %collective-permute-start.21 = (bf16[64,2304]{1,0:T(8,128)(2,1)S(1)}, bf16[64,2304]{1,0:T(8,128)(2,1)S(1)}, u32[]{:S(2)}, u32[]{:S(2)}) collective-permute-start(bf16[64,2304]{1,0:T(8,128)(2,1)S(1)} %get-tuple-element.64), channel_id=1, source_target_pairs={{0,4},{2,6},{4,0},{6,2},{1,5},{3,7},{5,1},{7,3},{8,12},{10,14},{12... | collective-permute-start | bytes 884744 | tf_op jit(solution)/shard_map/ppermute | solution.py:50
  225.4 15.9 %collective-permute-start.20 = (bf16[64,2304]{1,0:T(8,128)(2,1)S(1)}, bf16[64,2304]{1,0:T(8,128)(2,1)S(1)}, u32[]{:S(2)}, u32[]{:S(2)}) collective-permute-start(bf16[64,2304]{1,0:T(8,128)(2,1)S(1)} %get-tuple-element.64), channel_id=1, source_target_pairs={{0,2},{2,0},{4,6},{6,4},{1,3},{3,1},{5,7},{7,5},{8,10},{10,8},{12,... | collective-permute-start | bytes 884744 | tf_op jit(solution)/shard_map/ppermute | solution.py:50
  234.9 11.5 %collective-permute-start.22 = (bf16[64,2304]{1,0:T(8,128)(2,1)S(1)}, bf16[64,2304]{1,0:T(8,128)(2,1)S(1)}, u32[]{:S(2)}, u32[]{:S(2)}) collective-permute-start(bf16[64,2304]{1,0:T(8,128)(2,1)S(1)} %collective-permute-done.21), channel_id=1, source_target_pairs={{0,2},{2,0},{4,6},{6,4},{1,3},{3,1},{5,7},{7,5},{8,10},{10,8},{12,... | collective-permute-start | bytes 884744 | tf_op jit(solution)/shard_map/ppermute | solution.py:50
  270.6 9.9 %collective-permute-start.26 = (bf16[64,2304]{1,0:T(8,128)(2,1)S(1)}, bf16[64,2304]{1,0:T(8,128)(2,1)S(1)}, u32[]{:S(2)}, u32[]{:S(2)}) collective-permute-start(bf16[64,2304]{1,0:T(8,128)(2,1)S(1)} %get-tuple-element.86), channel_id=1, source_target_pairs={{0,2},{2,0},{4,6},{6,4},{1,3},{3,1},{5,7},{7,5},{8,10},{10,8},{12,... | collective-permute-start | bytes 884744 | tf_op jit(solution)/shard_map/ppermute | solution.py:50
  271.0 15.1 %collective-permute-start.25 = (bf16[64,2304]{1,0:T(8,128)(2,1)S(1)}, bf16[64,2304]{1,0:T(8,128)(2,1)S(1)}, u32[]{:S(2)}, u32[]{:S(2)}) collective-permute-start(bf16[64,2304]{1,0:T(8,128)(2,1)S(1)} %get-tuple-element.85), channel_id=1, source_target_pairs={{0,2},{2,0},{4,6},{6,4},{1,3},{3,1},{5,7},{7,5},{8,10},{10,8},{12,... | collective-permute-start | bytes 884744 | tf_op jit(solution)/shard_map/ppermute | solution.py:50
  280.6 17.7 %collective-permute-start.27 = (bf16[64,2304]{1,0:T(8,128)(2,1)S(1)}, bf16[64,2304]{1,0:T(8,128)(2,1)S(1)}, u32[]{:S(2)}, u32[]{:S(2)}) collective-permute-start(bf16[64,2304]{1,0:T(8,128)(2,1)S(1)} %fusion.67), channel_id=1, source_target_pairs={{0,4},{2,6},{4,0},{6,2},{1,5},{3,7},{5,1},{7,3},{8,12},{10,14},{12... | collective-permute-start | bytes 884744 | tf_op jit(solution)/shard_map/ppermute | solution.py:50
  300.3 10.0 %collective-permute-start.30 = (bf16[64,2304]{1,0:T(8,128)(2,1)S(1)}, bf16[64,2304]{1,0:T(8,128)(2,1)S(1)}, u32[]{:S(2)}, u32[]{:S(2)}) collective-permute-start(bf16[64,2304]{1,0:T(8,128)(2,1)S(1)} %get-tuple-element.58), channel_id=1, source_target_pairs={{0,4},{2,6},{4,0},{6,2},{1,5},{3,7},{5,1},{7,3},{8,12},{10,14},{12... | collective-permute-start | bytes 884744 | tf_op jit(solution)/shard_map/ppermute | solution.py:50
  300.3 16.2 %collective-permute-start.29 = (bf16[64,2304]{1,0:T(8,128)(2,1)S(1)}, bf16[64,2304]{1,0:T(8,128)(2,1)S(1)}, u32[]{:S(2)}, u32[]{:S(2)}) collective-permute-start(bf16[64,2304]{1,0:T(8,128)(2,1)S(1)} %get-tuple-element.58), channel_id=1, source_target_pairs={{0,2},{2,0},{4,6},{6,4},{1,3},{3,1},{5,7},{7,5},{8,10},{10,8},{12,... | collective-permute-start | bytes 884744 | tf_op jit(solution)/shard_map/ppermute | solution.py:50
  310.3 11.7 %collective-permute-start.31 = (bf16[64,2304]{1,0:T(8,128)(2,1)S(1)}, bf16[64,2304]{1,0:T(8,128)(2,1)S(1)}, u32[]{:S(2)}, u32[]{:S(2)}) collective-permute-start(bf16[64,2304]{1,0:T(8,128)(2,1)S(1)} %collective-permute-done.30), channel_id=1, source_target_pairs={{0,2},{2,0},{4,6},{6,4},{1,3},{3,1},{5,7},{7,5},{8,10},{10,8},{12,... | collective-permute-start | bytes 884744 | tf_op jit(solution)/shard_map/ppermute | solution.py:50
  331.5 251.9 %all-gather.10.cloned.1.call-start = ((), (), s32[]{:S(2)}) async-start(), calls=%async_computation.8 | async-start | bytes 6635520 | tf_op jit(solution)/shard_map/all_gather | solution.py:304
  391.2 192.2 %reduce-scatter.11.cloned.1.call-start = ((), (), s32[]{:S(2)}) async-start(), calls=%async_computation.7 | async-start | bytes 13271040 | tf_op jit(solution)/shard_map/reduce_scatter | solution.py:299
  411.6 226.7 %reduce-scatter.13.cloned.1.call-start = ((), (), s32[]{:S(2)}) async-start(), calls=%async_computation.11 | async-start | bytes 4423680
  424.1 37.3 %collective-permute-start.35 = (bf16[64,2304]{1,0:T(8,128)(2,1)S(1)}, bf16[64,2304]{1,0:T(8,128)(2,1)S(1)}, u32[]{:S(2)}, u32[]{:S(2)}) collective-permute-start(bf16[64,2304]{1,0:T(8,128)(2,1)S(1)} %get-tuple-element.84), channel_id=1, source_target_pairs={{0,2},{2,0},{4,6},{6,4},{1,3},{3,1},{5,7},{7,5},{8,10},{10,8},{12,... | collective-permute-start | bytes 884744 | tf_op jit(solution)/shard_map/ppermute | solution.py:50
  425.5 55.5 %collective-permute-start.34 = (bf16[64,2304]{1,0:T(8,128)(2,1)S(1)}, bf16[64,2304]{1,0:T(8,128)(2,1)S(1)}, u32[]{:S(2)}, u32[]{:S(2)}) collective-permute-start(bf16[64,2304]{1,0:T(8,128)(2,1)S(1)} %get-tuple-element.83), channel_id=1, source_target_pairs={{0,2},{2,0},{4,6},{6,4},{1,3},{3,1},{5,7},{7,5},{8,10},{10,8},{12,... | collective-permute-start | bytes 884744 | tf_op jit(solution)/shard_map/ppermute | solution.py:50
  461.5 33.5 %collective-permute-start.36 = (bf16[64,2304]{1,0:T(8,128)(2,1)S(1)}, bf16[64,2304]{1,0:T(8,128)(2,1)S(1)}, u32[]{:S(2)}, u32[]{:S(2)}) collective-permute-start(bf16[64,2304]{1,0:T(8,128)(2,1)S(1)} %fusion.65), channel_id=1, source_target_pairs={{0,4},{2,6},{4,0},{6,2},{1,5},{3,7},{5,1},{7,3},{8,12},{10,14},{12... | collective-permute-start | bytes 884744 | tf_op jit(solution)/shard_map/ppermute | solution.py:50
  497.8 19.8 %collective-permute-start.38 = (bf16[64,2304]{1,0:T(8,128)(2,1)S(1)}, bf16[64,2304]{1,0:T(8,128)(2,1)S(1)}, u32[]{:S(2)}, u32[]{:S(2)}) collective-permute-start(bf16[64,2304]{1,0:T(8,128)(2,1)S(1)} %get-tuple-element.53), channel_id=1, source_target_pairs={{0,4},{2,6},{4,0},{6,2},{1,5},{3,7},{5,1},{7,3},{8,12},{10,14},{12... | collective-permute-start | bytes 884744 | tf_op jit(solution)/shard_map/ppermute | solution.py:50
  497.8 22.0 %collective-permute-start.37 = (bf16[64,2304]{1,0:T(8,128)(2,1)S(1)}, bf16[64,2304]{1,0:T(8,128)(2,1)S(1)}, u32[]{:S(2)}, u32[]{:S(2)}) collective-permute-start(bf16[64,2304]{1,0:T(8,128)(2,1)S(1)} %get-tuple-element.53), channel_id=1, source_target_pairs={{0,2},{2,0},{4,6},{6,4},{1,3},{3,1},{5,7},{7,5},{8,10},{10,8},{12,... | collective-permute-start | bytes 884744 | tf_op jit(solution)/shard_map/ppermute | solution.py:50
  541.5 25.4 %collective-permute-start.41 = (bf16[2,1024,256]{2,1,0:T(8,128)(2,1)}, bf16[2,1024,256]{2,1,0:T(8,128)(2,1)S(1)}, u32[]{:S(2)}, u32[]{:S(2)}) collective-permute-start(bf16[2,1024,256]{2,1,0:T(8,128)(2,1)} %bitcast.126), channel_id=1, source_target_pairs={{0,2},{2,0},{4,6},{6,4},{1,3},{3,1},{5,7},{7,5},{8,10},{10,8},{12,... | collective-permute-start | bytes 3145736 | tf_op jit(solution)/shard_map/ppermute | solution.py:50
  567.4 9.3 %collective-permute-start.43 = (bf16[2,256,256]{2,1,0:T(8,128)(2,1)S(1)}, bf16[2,256,256]{2,1,0:T(8,128)(2,1)S(1)}, u32[]{:S(2)}, u32[]{:S(2)}) collective-permute-start(bf16[2,256,256]{2,1,0:T(8,128)(2,1)S(1)} %get-tuple-element.92), channel_id=1, source_target_pairs={{0,8},{8,0},{16,24},{24,16},{1,9},{9,1},{17,25},{25,17},{2,10},{10... | collective-permute-start | bytes 786440 | tf_op jit(solution)/shard_map/ppermute | solution.py:50
  570.8 9.8 %collective-permute-start.42 = (bf16[2,256,256]{2,1,0:T(8,128)(2,1)S(1)}, bf16[2,256,256]{2,1,0:T(8,128)(2,1)S(1)}, u32[]{:S(2)}, u32[]{:S(2)}) collective-permute-start(bf16[2,256,256]{2,1,0:T(8,128)(2,1)S(1)} %get-tuple-element.91), channel_id=1, source_target_pairs={{0,8},{8,0},{16,24},{24,16},{1,9},{9,1},{17,25},{25,17},{2,10},{10... | collective-permute-start | bytes 786440 | tf_op jit(solution)/shard_map/ppermute | solution.py:50
  589.4 203.3 %all-gather.12.cloned.1.call-start = ((), (), s32[]{:S(2)}) async-start(), calls=%async_computation.9 | async-start | bytes 13271040 | tf_op jit(solution)/shard_map/all_gather | solution.py:304
  590.2 275.7 %all-gather.14.cloned.1.call-start = ((), (), s32[]{:S(2)}) async-start(), calls=%async_computation.10 | async-start | bytes 4423680 | tf_op jit(solution)/shard_map/all_gather | solution.py:304
  597.9 12.7 %collective-permute-start.47 = (bf16[64,2304]{1,0:T(8,128)(2,1)S(1)}, bf16[64,2304]{1,0:T(8,128)(2,1)S(1)}, u32[]{:S(2)}, u32[]{:S(2)}) collective-permute-start(bf16[64,2304]{1,0:T(8,128)(2,1)S(1)} %get-tuple-element.82), channel_id=1, source_target_pairs={{0,2},{2,0},{4,6},{6,4},{1,3},{3,1},{5,7},{7,5},{8,10},{10,8},{12,... | collective-permute-start | bytes 884744 | tf_op jit(solution)/shard_map/ppermute | solution.py:50
  600.1 197.0 %collective-permute-start.46 = (bf16[64,2304]{1,0:T(8,128)(2,1)}, bf16[64,2304]{1,0:T(8,128)(2,1)}, u32[]{:S(2)}, u32[]{:S(2)}) collective-permute-start(bf16[64,2304]{1,0:T(8,128)(2,1)} %get-tuple-element.81), channel_id=1, source_target_pairs={{0,2},{2,0},{4,6},{6,4},{1,3},{3,1},{5,7},{7,5},{8,10},{10,8},{12,... | collective-permute-start | bytes 884744 | tf_op jit(solution)/shard_map/ppermute | solution.py:50
  611.4 185.7 %collective-permute-start.48 = (bf16[64,2304]{1,0:T(8,128)(2,1)}, bf16[64,2304]{1,0:T(8,128)(2,1)}, u32[]{:S(2)}, u32[]{:S(2)}) collective-permute-start(bf16[64,2304]{1,0:T(8,128)(2,1)} %fusion.63), channel_id=1, source_target_pairs={{0,4},{2,6},{4,0},{6,2},{1,5},{3,7},{5,1},{7,3},{8,12},{10,14},{12... | collective-permute-start | bytes 884744 | tf_op jit(solution)/shard_map/ppermute | solution.py:50
  798.7 14.3 %collective-permute-start.28 = (bf16[64,2304]{1,0:T(8,128)(2,1)}, bf16[64,2304]{1,0:T(8,128)(2,1)S(1)}, u32[]{:S(2)}, u32[]{:S(2)}) collective-permute-start(bf16[64,2304]{1,0:T(8,128)(2,1)} %get-tuple-element.93), channel_id=1, source_target_pairs={{0,1},{1,0},{2,3},{3,2},{4,5},{5,4},{6,7},{7,6},{8,9},{9,8},{10,11... | collective-permute-start | bytes 884744 | tf_op jit(solution)/shard_map/ppermute | solution.py:50
  806.6 24.6 %collective-permute-start.49 = (f32[64,2304]{1,0:T(8,128)S(1)}, f32[64,2304]{1,0:T(8,128)S(1)}, u32[]{:S(2)}, u32[]{:S(2)}) collective-permute-start(f32[64,2304]{1,0:T(8,128)S(1)} %fusion.59), channel_id=1, source_target_pairs={{0,1},{1,0},{2,3},{3,2},{4,5},{5,4},{6,7},{7,6},{8,9},{9,8},{10,11... | collective-permute-start | bytes 1769480 | tf_op jit(solution)/shard_map/ppermute | solution.py:50
  815.4 15.2 %collective-permute-start.54 = (f32[4,2304]{1,0:T(4,128)S(1)}, f32[4,2304]{1,0:T(4,128)S(1)}, u32[]{:S(2)}, u32[]{:S(2)}) collective-permute-start(f32[4,2304]{1,0:T(4,128)S(1)} %add.286), channel_id=1, source_target_pairs={{0,16},{8,24},{16,0},{24,8},{1,17},{9,25},{17,1},{25,9},{2,18},{10... | collective-permute-start | bytes 110600 | tf_op jit(solution)/shard_map/ppermute | solution.py:50
  (79 other events, 1497.1 us)
Sparse Core Ops, SparseCore 0:
  12.5 21.7 reduce-scatter.6
  391.4 123.5 all-gather.9
  591.9 200.7 all-gather.11
  795.0 70.7 all-gather.13
Sparse Core Ops, SparseCore 1:
  25.5 212.6 all-gather.7
  331.6 59.6 reduce-scatter.8
  411.7 104.4 reduce-scatter.10
  589.5 48.8 reduce-scatter.12
